TPU v7x, 32 devices: a whole 2x2x4 slice. The times are simulated.
32 devices in a mesh: var: 16 (over z, y, core), samp: 2 (over x).
Axes of the slice: x: 2, y: 2, z: 4, core: 2. Of those that a mesh axis runs over, the one named last changes fastest.
Arguments:
- genotypes: bfloat16 [4096, 12288], P('samp', 'var'), may hold values from -6 to 6
- marginal: float32 [12288, 1024], P('var', 'samp'), may hold values from -6 to 6
- start_effects: float32 [12288, 1024], P('var', 'samp'), may hold values from -5 to 5
- thresholds: float32 [1024], P('samp'), may hold values from 0.02 to 0.5
Outputs:
- shrunk_effects: float32 [12288, 1024], P('var', 'samp')
All inputs are finite; a program needn't handle non-finite values.
Results may differ from a plain program's by a relative error of at most 0.0003.
Values may be sent and summed in bfloat16 or wider, within the bound.
A program may use at most 64 MiB of HBM per device.

v0:
```python
import functools

import jax
import jax.numpy as jnp
from jax import lax
from jax.experimental import pallas as pl
from jax.experimental.pallas import tpu as pltpu
from jax.sharding import PartitionSpec as P

TILE = 256
HALF = TILE // 2
SWEEPS = 2
CHUNKS = 4
TINY = 2.0**-126
VMEM_BYTES = 40 * 1024 * 1024
LD_SCALE = 1024.0

shrinkage = 0.2
MESH = pl.DeviceIdType.MESH
F32 = jnp.float32
BF16 = jnp.bfloat16


def encode(value):
    square = value * value
    fourth = square * square
    eighth = fourth * fourth
    return jnp.where(value < 0, -eighth, eighth).astype(BF16)


def decode(code):
    code = code.astype(F32)
    size = jnp.abs(code)
    fourth_root = lax.rsqrt(lax.rsqrt(jnp.maximum(size, TINY)))
    root = jnp.where(size < TINY, 0.0, fourth_root * lax.rsqrt(fourth_root))
    return jnp.where(code < 0, -root, root)


def split(value):
    high = value.astype(BF16)
    return high, (value - high.astype(F32)).astype(BF16)


def iota_pair(size):
    row = lax.broadcasted_iota(jnp.int32, (size, size), 0)
    col = lax.broadcasted_iota(jnp.int32, (size, size), 1)
    return row, col


def pack_symmetric(tile):
    row, col = iota_pair(HALF)
    mixed = jnp.where(row < col, tile[:HALF, :HALF], tile[HALF:, HALF:])
    return jnp.concatenate([mixed, tile[:HALF, HALF:]], axis=1)


def unpack_symmetric(packed):
    row, col = iota_pair(HALF)
    mixed, corner = packed[:, :HALF], packed[:, HALF:]
    upper = jnp.where(row < col, mixed, 0.0)
    lower = jnp.where(row > col, mixed, 0.0)
    first = jnp.concatenate([upper + upper.T, corner], axis=1)
    second = jnp.concatenate([corner.T, lower + lower.T], axis=1)
    return jnp.concatenate([first, second], axis=0)


def gram(left, right):
    return lax.dot_general(left, right, (((0,), (0,)), ((), ())), preferred_element_type=F32)


def kernel(
    tiles, var_size, samp_size, inv_total,
    geno_hbm, marg_hbm, start_hbm, limit_hbm, out,
    geno, halo, marg, start, limit_row, own, code, got, diag, diag_got,
    band_hi, band_lo, eff_hi, eff_lo, edge_code, edge_got, cross_code, cross_got,
    load_sem, geno_send, geno_recv, part_send, part_recv, cross_sem, edge_send, edge_recv,
):
    var = lax.axis_index("var")
    samp = lax.axis_index("samp")
    has_prev = var > 0
    has_next = var < var_size - 1
    prev, following = var - 1, var + 1
    peers = [lax.rem(samp + k, samp_size) for k in range(1, samp_size)]
    last = tiles - 1
    pieces, width = edge_code.shape[2], edge_code.shape[4]
    slices = [slice(c * width, (c + 1) * width) for c in range(pieces)]

    step = HALF + TILE
    cross_at = tiles * step - TILE
    total_rows = cross_at + TILE

    loads = []
    for t in range(tiles):
        cols = pl.ds(t * TILE, TILE)
        loads.append(pltpu.make_async_copy(geno_hbm.at[:, cols], geno.at[:, cols], load_sem.at[t]))
    loads.append(pltpu.make_async_copy(start_hbm, start, load_sem.at[tiles]))
    loads.append(pltpu.make_async_copy(marg_hbm, marg, load_sem.at[tiles + 1]))
    loads.append(pltpu.make_async_copy(limit_hbm, limit_row, load_sem.at[tiles + 2]))
    for copy in loads:
        copy.start()

    barrier = pltpu.get_barrier_semaphore()

    @pl.when(has_prev)
    def _():
        pl.semaphore_signal(barrier, inc=1, device_id={"var": prev}, device_id_type=MESH)

    @pl.when(has_next)
    def _():
        pl.semaphore_signal(barrier, inc=1, device_id={"var": following}, device_id_type=MESH)

    for peer in peers:
        pl.semaphore_signal(barrier, inc=1, device_id={"samp": peer}, device_id_type=MESH)
    pl.semaphore_wait(
        barrier, len(peers) + has_prev.astype(jnp.int32) + has_next.astype(jnp.int32)
    )

    depth = geno.shape[0] // CHUNKS

    def geno_copy(chunk):
        rows = pl.ds(chunk * depth, depth)
        return pltpu.make_async_remote_copy(
            src_ref=geno_hbm.at[rows, pl.ds(last * TILE, TILE)], dst_ref=halo.at[rows],
            send_sem=geno_send.at[chunk], recv_sem=geno_recv.at[chunk],
            device_id={"var": following}, device_id_type=MESH,
        )

    @pl.when(has_next)
    def _():
        for chunk in range(CHUNKS):
            geno_copy(chunk).start()

    def part_copy(k, message):
        if message == tiles + 1:
            src, dst = diag, diag_got.at[k]
        else:
            begin = message * step if message < tiles else cross_at
            rows = pl.ds(begin, TILE if message == tiles else HALF if message == last else step)
            src, dst = code.at[rows], got.at[k, rows]
        return pltpu.make_async_remote_copy(
            src_ref=src, dst_ref=dst,
            send_sem=part_send.at[k, message], recv_sem=part_recv.at[k, message],
            device_id={"samp": peers[k]}, device_id_type=MESH,
        )

    def send_part(message):
        for k in range(len(peers)):
            part_copy(k, message).start()

    diag[...] = jnp.zeros_like(diag)
    row, col = iota_pair(TILE)
    on_diagonal = row == col

    for t in range(tiles):
        if t == 0:
            loads[0].wait()
        if t + 1 < tiles:
            loads[t + 1].wait()
        reach = min(t + 2, tiles) * TILE
        product = gram(geno[:, t * TILE : (t + 1) * TILE], geno[:, t * TILE : reach])
        product = product * (inv_total * LD_SCALE)
        block = product[:, :TILE]
        diag[pl.ds(t, 1), :] = jnp.sum(jnp.where(on_diagonal, block, 0.0), axis=0, keepdims=True)
        begin = t * step
        packed = pack_symmetric(block)
        own[begin : begin + HALF] = packed
        code[begin : begin + HALF] = encode(packed)
        if t + 1 < tiles:
            beside = product[:, TILE:]
            own[begin + HALF : begin + step] = beside
            code[begin + HALF : begin + step] = encode(beside)
        if t == last:
            send_part(tiles + 1)
        send_part(t)

    for copy in loads[tiles:]:
        copy.wait()
    everything = slice(0, pieces * width)

    def place(sweep, slot, value, cols=everything):
        high, low = split(value)
        eff_hi[sweep, slot * TILE : (slot + 1) * TILE, cols] = high
        eff_lo[sweep, slot * TILE : (slot + 1) * TILE, cols] = low

    def edge_copy(sweep, side, piece):
        return pltpu.make_async_remote_copy(
            src_ref=edge_code.at[sweep, side, piece], dst_ref=edge_got.at[sweep, side, piece],
            send_sem=edge_send.at[sweep, side, piece], recv_sem=edge_recv.at[sweep, side, piece],
            device_id={"var": following if side else prev}, device_id_type=MESH,
        )

    def send_edge(sweep, side, piece):
        @pl.when(has_next if side else has_prev)
        def _():
            edge_copy(sweep, side, piece).start()

    def take_edge(sweep, side, piece):
        slot = 0 if side else tiles + 1
        exists = has_prev if side else has_next

        @pl.when(exists)
        def _():
            edge_copy(sweep, side, piece).wait_recv()
            place(sweep, slot, decode(edge_got[sweep, side, piece]), slices[piece])

        @pl.when(jnp.logical_not(exists))
        def _():
            place(sweep, slot, jnp.zeros((TILE, width), F32), slices[piece])

    for side, rows in ((1, slice(last * TILE, tiles * TILE)), (0, slice(0, TILE))):
        for piece in range(pieces):
            edge_code[0, side, piece] = encode(start[rows, slices[piece]])
            if side:
                send_edge(0, side, piece)
    for t in range(tiles):
        place(0, t + 1, start[t * TILE : (t + 1) * TILE])

    def summed(begin, size):
        value = own[begin : begin + size]
        for k in range(len(peers)):
            value = value + decode(got[k, begin : begin + size])
        return value

    def put(tile, slot, value):
        high, low = split(value)
        band_hi[tile, :, slot * TILE : (slot + 1) * TILE] = high
        band_lo[tile, :, slot * TILE : (slot + 1) * TILE] = low

    def applied(sweep, tile, first, count, cols=everything):
        across = slice(first * TILE, (first + count) * TILE)
        rows = slice((tile + first) * TILE, (tile + first + count) * TILE)
        high, low = band_hi[tile, :, across], band_lo[tile, :, across]
        near, rest = eff_hi[sweep, rows, cols], eff_lo[sweep, rows, cols]
        dot = functools.partial(jnp.dot, preferred_element_type=F32)
        return dot(high, near) + (dot(high, rest) + dot(low, near))

    def add_tile(t):
        for k in range(len(peers)):
            part_copy(k, t).wait_recv()
        begin = t * step
        put(t, 1, unpack_symmetric(summed(begin, HALF)) * (1.0 / LD_SCALE))
        if t + 1 < tiles:
            beside = summed(begin + HALF, TILE) * (1.0 / LD_SCALE)
            put(t, 2, beside)
            put(t + 1, 0, beside.T)

    def cross_step(now):
        @pl.when(jnp.logical_and(has_prev, now))
        def _():
            crossing = jnp.zeros((TILE, TILE), F32)
            for chunk in range(CHUNKS):
                rows = slice(chunk * depth, (chunk + 1) * depth)
                geno_copy(chunk).wait_recv()
                if chunk == CHUNKS - 1:
                    for piece in range(pieces):
                        edge_copy(0, 0, piece).start()
                crossing = crossing + gram(halo[rows], geno[rows, :TILE])
            crossing = crossing * (inv_total * LD_SCALE)
            own[cross_at:total_rows] = crossing
            code[cross_at:total_rows] = encode(crossing)
            send_part(tiles)

    nearby = lax.rem(var, 2) == 1
    cross_step(nearby)
    for t in range(last):
        add_tile(t)
    near_first = applied(0, 0, 1, 2)

    cross_step(jnp.logical_not(nearby))
    add_tile(last)
    for k in range(len(peers)):
        part_copy(k, tiles + 1).wait_recv()
    keep = []
    for t in range(tiles):
        whole = diag[pl.ds(t, 1), :]
        for k in range(len(peers)):
            whole = whole + diag_got[k, pl.ds(t, 1), :]
        column = jnp.sum(jnp.where(on_diagonal, whole, 0.0), axis=1, keepdims=True) * (1.0 / LD_SCALE)
        keep.append(1.0 / ((1.0 - shrinkage) * column + shrinkage))
    limit = limit_row[...]

    def finish(tile, combined, cols=everything):
        adjusted = marg[tile * TILE : (tile + 1) * TILE, cols] - (1.0 - shrinkage) * combined
        bound = limit[:, cols]
        return (adjusted - jnp.clip(adjusted, -bound, bound)) * keep[tile]

    for t in range(1, tiles - 1):
        place(1, t + 1, finish(t, applied(0, t, 0, 3)))
    near_last = applied(0, last, 0, 2)

    def back_copy():
        return pltpu.make_async_remote_copy(
            src_ref=cross_code, dst_ref=cross_got,
            send_sem=cross_sem.at[0], recv_sem=cross_sem.at[1],
            device_id={"var": prev}, device_id_type=MESH,
        )

    @pl.when(has_prev)
    def _():
        for k in range(len(peers)):
            part_copy(k, tiles).wait_recv()
        crossing = summed(cross_at, TILE)
        cross_code[...] = encode(crossing)
        back_copy().start()
        put(0, 0, crossing.T * (1.0 / LD_SCALE))

    @pl.when(jnp.logical_not(has_prev))
    def _():
        put(0, 0, jnp.zeros((TILE, TILE), F32))

    for piece, cols in enumerate(slices):
        take_edge(0, 1, piece)
        value = finish(0, near_first[:, cols] + applied(0, 0, 0, 1, cols), cols)
        edge_code[1, 0, piece] = encode(value)
        send_edge(1, 0, piece)
        place(1, 1, value, cols)

    for piece in range(pieces):
        take_edge(0, 0, piece)

    @pl.when(has_next)
    def _():
        back_copy().wait_recv()
        put(last, 2, decode(cross_got[...]) * (1.0 / LD_SCALE))

    @pl.when(jnp.logical_not(has_next))
    def _():
        put(last, 2, jnp.zeros((TILE, TILE), F32))

    for piece, cols in enumerate(slices):
        value = finish(last, near_last[:, cols] + applied(0, last, 2, 1, cols), cols)
        edge_code[1, 1, piece] = encode(value)
        send_edge(1, 1, piece)
        place(1, tiles, value, cols)

    for t in range(1, tiles - 1):
        out[t * TILE : (t + 1) * TILE] = finish(t, applied(1, t, 0, 3))
    near_last = applied(1, last, 0, 2)
    near_first = applied(1, 0, 1, 2)
    for piece, cols in enumerate(slices):
        take_edge(1, 0, piece)
        combined = near_last[:, cols] + applied(1, last, 2, 1, cols)
        out[last * TILE : tiles * TILE, cols] = finish(last, combined, cols)
    for piece, cols in enumerate(slices):
        take_edge(1, 1, piece)
        combined = near_first[:, cols] + applied(1, 0, 0, 1, cols)
        out[:TILE, cols] = finish(0, combined, cols)

    for k in range(len(peers)):
        for message in list(range(tiles)) + [tiles + 1]:
            part_copy(k, message).wait_send()

    @pl.when(has_prev)
    def _():
        for k in range(len(peers)):
            part_copy(k, tiles).wait_send()
        back_copy().wait_send()
        for sweep in range(SWEEPS):
            for piece in range(pieces):
                edge_copy(sweep, 0, piece).wait_send()

    @pl.when(has_next)
    def _():
        for chunk in range(CHUNKS):
            geno_copy(chunk).wait_send()
        for sweep in range(SWEEPS):
            for piece in range(pieces):
                edge_copy(sweep, 1, piece).wait_send()


def local(genotypes, marginal, start_effects, thresholds):
    samples, variants = genotypes.shape
    traits = marginal.shape[1]
    tiles = variants // TILE
    var_size, samp_size = lax.axis_size("var"), lax.axis_size("samp")
    others = samp_size - 1
    rows = tiles * (HALF + TILE)
    pieces = 1
    width = traits // pieces
    dma = pltpu.SemaphoreType.DMA
    body = functools.partial(
        kernel, tiles, var_size, samp_size, 1.0 / (samples * samp_size)
    )
    return pl.pallas_call(
        body,
        out_shape=jax.ShapeDtypeStruct((variants, traits), F32),
        in_specs=[pl.BlockSpec(memory_space=pltpu.HBM)] * 4,
        out_specs=pl.BlockSpec(memory_space=pltpu.VMEM),
        scratch_shapes=[
            pltpu.VMEM((samples, variants), BF16),
            pltpu.VMEM((samples, TILE), BF16),
            pltpu.VMEM((variants, traits), F32),
            pltpu.VMEM((variants, traits), F32),
            pltpu.VMEM((1, traits), F32),
            pltpu.VMEM((rows, TILE), F32),
            pltpu.VMEM((rows, TILE), BF16),
            pltpu.VMEM((others, rows, TILE), BF16),
            pltpu.VMEM((8, TILE), F32),
            pltpu.VMEM((others, 8, TILE), F32),
            pltpu.VMEM((tiles, TILE, 3 * TILE), BF16),
            pltpu.VMEM((tiles, TILE, 3 * TILE), BF16),
            pltpu.VMEM((SWEEPS, (tiles + 2) * TILE, traits), BF16),
            pltpu.VMEM((SWEEPS, (tiles + 2) * TILE, traits), BF16),
            pltpu.VMEM((SWEEPS, 2, pieces, TILE, width), BF16),
            pltpu.VMEM((SWEEPS, 2, pieces, TILE, width), BF16),
            pltpu.VMEM((TILE, TILE), BF16),
            pltpu.VMEM((TILE, TILE), BF16),
            dma((tiles + 3,)),
            dma((CHUNKS,)),
            dma((CHUNKS,)),
            dma((others, tiles + 2)),
            dma((others, tiles + 2)),
            dma((2,)),
            dma((SWEEPS, 2, pieces)),
            dma((SWEEPS, 2, pieces)),
        ],
        compiler_params=pltpu.CompilerParams(
            collective_id=0, has_side_effects=True, vmem_limit_bytes=VMEM_BYTES
        ),
    )(*(
        pltpu.with_memory_space_constraint(array, pltpu.HBM)
        for array in (genotypes, marginal, start_effects, thresholds[None, :])
    ))


def solution(mesh):
    in_specs = (P("samp", "var"), P("var", "samp"), P("var", "samp"), P("samp"))
    out_specs = P("var", "samp")
    return jax.shard_map(local, mesh=mesh, in_specs=in_specs, out_specs=out_specs, check_vma=False)
```

profile of v0, /device:TPU:4, one launch (start us, length us, event | category | flops | bytes accessed | tf_op | source)
XLA Modules:
  0.0 32.5 jit_solution(16916876671941277037)
XLA Ops:
  0.0 31.4 %shard_map.46 = f32[768,512]{1,0:T(8,128)S(1)} custom-call(bf16[2048,768]{1,0:T(8,128)(2,1)} %geno_hbm.1, f32[768,512]{1,0:T(8,128)} %marg_hbm.1, f32[768,512]{1,0:T(8,128)} %start_hbm.1, f32[1,512]{1,0:T(1,128)} %bitcast.1), custom_call_target="tpu_custom_call" | custom-call | tf_op jit(solution)/shard_map/pallas_call | solution.py:383
  31.4 1.1 %copy.6 = f32[768,512]{1,0:T(8,128)} copy(f32[768,512]{1,0:T(8,128)S(1)} %shard_map.46) | data formatting | bytes 3145728
where the time goes:
time: 32.7 us; the launch traced here: 32.5 us
  Pallas kernels  31.4 us (96%)
  local copies, waits for them, and re-layouts  1.15 us (4%)
    pallas_call x1, Pallas kernels, local(): pl.pallas_call(body, out_shape=jax.ShapeDtypeStruct((variants, traits), F...  31.4 us
    unnamed x1, local copies, waits for them, and re-layouts  1.15 us

commit v1 on v0

v1 whole, which is shorter than its diff:
```python
import functools

import jax
import jax.numpy as jnp
from jax import lax
from jax.experimental import pallas as pl
from jax.experimental.pallas import tpu as pltpu
from jax.sharding import PartitionSpec as P

TILE = 256
HALF = TILE // 2
SWEEPS = 2
CHUNKS = 4
BACK_FIRST = 2
BACK_LAST = 4
TINY = 2.0**-126
VMEM_BYTES = 40 * 1024 * 1024
LD_SCALE = 1024.0

shrinkage = 0.2
MESH = pl.DeviceIdType.MESH
F32 = jnp.float32
BF16 = jnp.bfloat16


def encode(value):
    square = value * value
    fourth = square * square
    eighth = fourth * fourth
    return jnp.where(value < 0, -eighth, eighth).astype(BF16)


def decode(code):
    code = code.astype(F32)
    size = jnp.abs(code)
    fourth_root = lax.rsqrt(lax.rsqrt(jnp.maximum(size, TINY)))
    root = jnp.where(size < TINY, 0.0, fourth_root * lax.rsqrt(fourth_root))
    return jnp.where(code < 0, -root, root)


def encode_wide(value):
    square = value * value
    fourth = square * square
    return jnp.where(value < 0, -fourth, fourth).astype(BF16)


def decode_wide(code):
    code = code.astype(F32)
    size = jnp.abs(code)
    root = jnp.where(size < TINY, 0.0, lax.rsqrt(lax.rsqrt(jnp.maximum(size, TINY))))
    return jnp.where(code < 0, -root, root)


def split(value):
    high = value.astype(BF16)
    return high, (value - high.astype(F32)).astype(BF16)


def iota_pair(size):
    row = lax.broadcasted_iota(jnp.int32, (size, size), 0)
    col = lax.broadcasted_iota(jnp.int32, (size, size), 1)
    return row, col


def pack_symmetric(tile):
    row, col = iota_pair(HALF)
    mixed = jnp.where(row < col, tile[:HALF, :HALF], tile[HALF:, HALF:])
    return jnp.concatenate([mixed, tile[:HALF, HALF:]], axis=1)


def unpack_symmetric(packed):
    row, col = iota_pair(HALF)
    mixed, corner = packed[:, :HALF], packed[:, HALF:]
    upper = jnp.where(row < col, mixed, 0.0)
    lower = jnp.where(row > col, mixed, 0.0)
    first = jnp.concatenate([upper + upper.T, corner], axis=1)
    second = jnp.concatenate([corner.T, lower + lower.T], axis=1)
    return jnp.concatenate([first, second], axis=0)


def gram(left, right):
    return lax.dot_general(left, right, (((0,), (0,)), ((), ())), preferred_element_type=F32)


def kernel(
    tiles, var_size, samp_size, inv_total,
    geno_hbm, marg_hbm, start_hbm, limit_hbm, out,
    geno, halo, marg, start, limit_row, own, code, got, diag, diag_got,
    band_hi, band_lo, eff_hi, eff_lo, cross_hi, cross_lo, first_term,
    early_code, early_got, tail_diag, tail_got, back_code, back_got,
    load_sem, geno_send, geno_recv, part_send, part_recv,
    early_send, early_recv, back_send, back_recv,
):
    var = lax.axis_index("var")
    samp = lax.axis_index("samp")
    has_prev = var > 0
    has_next = var < var_size - 1
    prev, following = var - 1, var + 1
    peers = [lax.rem(samp + k, samp_size) for k in range(1, samp_size)]
    last = tiles - 1
    tail = slice(last * TILE, tiles * TILE)

    step = HALF + TILE
    cross_at = tiles * step - TILE
    halves = range(2)
    diag_message = tiles + 2

    loads = []
    for t in range(tiles):
        cols = pl.ds(t * TILE, TILE)
        loads.append(pltpu.make_async_copy(geno_hbm.at[:, cols], geno.at[:, cols], load_sem.at[t]))
    loads.append(pltpu.make_async_copy(start_hbm, start, load_sem.at[tiles]))
    loads.append(pltpu.make_async_copy(marg_hbm, marg, load_sem.at[tiles + 1]))
    loads.append(pltpu.make_async_copy(limit_hbm, limit_row, load_sem.at[tiles + 2]))
    for copy in loads:
        copy.start()

    barrier = pltpu.get_barrier_semaphore()

    @pl.when(has_prev)
    def _():
        pl.semaphore_signal(barrier, inc=1, device_id={"var": prev}, device_id_type=MESH)

    @pl.when(has_next)
    def _():
        pl.semaphore_signal(barrier, inc=1, device_id={"var": following}, device_id_type=MESH)

    for peer in peers:
        pl.semaphore_signal(barrier, inc=1, device_id={"samp": peer}, device_id_type=MESH)
    pl.semaphore_wait(
        barrier, len(peers) + has_prev.astype(jnp.int32) + has_next.astype(jnp.int32)
    )

    depth = geno.shape[0] // CHUNKS
    chunks = [(half, chunk) for half in halves for chunk in range(CHUNKS)]

    def geno_copy(half, chunk):
        rows = pl.ds(chunk * depth, depth)
        return pltpu.make_async_remote_copy(
            src_ref=geno_hbm.at[rows, pl.ds(last * TILE + half * HALF, HALF)],
            dst_ref=halo.at[rows, pl.ds(half * HALF, HALF)],
            send_sem=geno_send.at[half, chunk], recv_sem=geno_recv.at[half, chunk],
            device_id={"var": following}, device_id_type=MESH,
        )

    @pl.when(has_next)
    def _():
        for half, chunk in chunks:
            geno_copy(half, chunk).start()

    def part_copy(k, message):
        if message == diag_message:
            src, dst = diag, diag_got.at[k]
        else:
            if message < tiles:
                rows = pl.ds(message * step, HALF if message == last else step)
            else:
                rows = pl.ds(cross_at + (message - tiles) * HALF, HALF)
            src, dst = code.at[rows], got.at[k, rows]
        return pltpu.make_async_remote_copy(
            src_ref=src, dst_ref=dst,
            send_sem=part_send.at[k, message], recv_sem=part_recv.at[k, message],
            device_id={"samp": peers[k]}, device_id_type=MESH,
        )

    def send_part(message):
        for k in range(len(peers)):
            part_copy(k, message).start()

    def take_part(message):
        for k in range(len(peers)):
            part_copy(k, message).wait_recv()

    diag[...] = jnp.zeros_like(diag)
    row, col = iota_pair(TILE)
    on_diagonal = row == col

    for t in range(tiles):
        if t == 0:
            loads[0].wait()
        if t + 1 < tiles:
            loads[t + 1].wait()
        reach = min(t + 2, tiles) * TILE
        product = gram(geno[:, t * TILE : (t + 1) * TILE], geno[:, t * TILE : reach])
        product = product * (inv_total * LD_SCALE)
        block = product[:, :TILE]
        diag[pl.ds(t, 1), :] = jnp.sum(jnp.where(on_diagonal, block, 0.0), axis=0, keepdims=True)
        begin = t * step
        packed = pack_symmetric(block)
        own[begin : begin + HALF] = packed
        code[begin : begin + HALF] = encode(packed)
        if t + 1 < tiles:
            beside = product[:, TILE:]
            own[begin + HALF : begin + step] = beside
            code[begin + HALF : begin + step] = encode(beside)
        if t == last:
            send_part(diag_message)
        send_part(t)

    for copy in loads[tiles:]:
        copy.wait()

    def place(sweep, slot, value, first=0):
        begin = slot * TILE + first
        high, low = split(value)
        eff_hi[sweep, begin : begin + value.shape[0]] = high
        eff_lo[sweep, begin : begin + value.shape[0]] = low

    early = [(early_code.at[k], early_got.at[k]) for k in range(2)] + [(tail_diag, tail_got)]

    def early_copy(k):
        src, dst = early[k]
        return pltpu.make_async_remote_copy(
            src_ref=src, dst_ref=dst, send_sem=early_send.at[k], recv_sem=early_recv.at[k],
            device_id={"var": following}, device_id_type=MESH,
        )

    def send_early(k):
        @pl.when(has_next)
        def _():
            early_copy(k).start()

    early_code[0] = encode(start[tail])
    send_early(0)
    for t in range(tiles):
        place(0, t + 1, start[t * TILE : (t + 1) * TILE])

    def summed(begin, size):
        value = own[begin : begin + size]
        for k in range(len(peers)):
            value = value + decode(got[k, begin : begin + size])
        return value

    def put(tile, slot, value, first=0):
        high, low = split(value)
        begin = slot * TILE + first
        band_hi[tile, :, begin : begin + value.shape[1]] = high
        band_lo[tile, :, begin : begin + value.shape[1]] = low

    dot = functools.partial(jnp.dot, preferred_element_type=F32)

    def applied(sweep, tile, first, count):
        across = slice(first * TILE, (first + count) * TILE)
        rows = slice((tile + first) * TILE, (tile + first + count) * TILE)
        high, low = band_hi[tile, :, across], band_lo[tile, :, across]
        near, rest = eff_hi[sweep, rows], eff_lo[sweep, rows]
        return dot(high, near) + (dot(high, rest) + dot(low, near))

    def add_tile(t):
        take_part(t)
        begin = t * step
        put(t, 1, unpack_symmetric(summed(begin, HALF)) * (1.0 / LD_SCALE))
        if t + 1 < tiles:
            beside = summed(begin + HALF, TILE) * (1.0 / LD_SCALE)
            put(t, 2, beside)
            put(t + 1, 0, beside.T)

    def cross_step(now):
        @pl.when(jnp.logical_and(has_prev, now))
        def _():
            for half in halves:
                crossing = jnp.zeros((HALF, TILE), F32)
                for chunk in range(CHUNKS):
                    rows = slice(chunk * depth, (chunk + 1) * depth)
                    geno_copy(half, chunk).wait_recv()
                    crossing = crossing + gram(
                        halo[rows, half * HALF : (half + 1) * HALF], geno[rows, :TILE]
                    )
                crossing = crossing * (inv_total * LD_SCALE)
                begin = cross_at + half * HALF
                own[begin : begin + HALF] = crossing
                code[begin : begin + HALF] = encode(crossing)
                send_part(tiles + half)

    nearby = lax.rem(var, 2) == 1
    cross_step(nearby)
    for t in range(tiles):
        add_tile(t)
    take_part(diag_message)

    def keep_of(whole):
        column = jnp.sum(jnp.where(on_diagonal, whole, 0.0), axis=1, keepdims=True) * (1.0 / LD_SCALE)
        return 1.0 / ((1.0 - shrinkage) * column + shrinkage)

    keep = []
    for t in range(tiles):
        whole = diag[pl.ds(t, 1), :]
        for k in range(len(peers)):
            whole = whole + diag_got[k, pl.ds(t, 1), :]
        keep.append(keep_of(whole))
        if t == last:
            tail_diag[...] = jnp.broadcast_to(whole, tail_diag.shape)
    limit = limit_row[...]

    def adjust(tile, combined, rows=slice(0, TILE)):
        shift = slice(tile * TILE + rows.start, tile * TILE + rows.stop)
        return (marg[shift] - (1.0 - shrinkage) * combined) * keep[tile][rows]

    def soften(value, scale):
        bound = limit * scale
        return value - jnp.clip(value, -bound, bound)

    def finish(tile, combined, rows=slice(0, TILE)):
        return soften(adjust(tile, combined, rows), keep[tile][rows])

    near_last = applied(0, last, 0, 2)
    early_code[1] = encode(adjust(last, near_last))
    send_early(2)
    send_early(1)
    near_first = applied(0, 0, 1, 2)
    for t in range(1, last):
        place(1, t + 1, finish(t, applied(0, t, 0, 3)))

    cross_step(jnp.logical_not(nearby))

    sizes = (BACK_FIRST, BACK_LAST)
    places = [(sweep, piece) for sweep in range(SWEEPS) for piece in range(sizes[sweep])]

    def piece_rows(sweep, piece):
        size = TILE // sizes[sweep]
        return slice(piece * size, (piece + 1) * size)

    def back_copy(sweep, piece):
        rows = piece_rows(sweep, piece)
        return pltpu.make_async_remote_copy(
            src_ref=back_code.at[sweep, pl.ds(rows.start, rows.stop - rows.start)],
            dst_ref=back_got.at[sweep, pl.ds(rows.start, rows.stop - rows.start)],
            send_sem=back_send.at[sweep, piece], recv_sem=back_recv.at[sweep, piece],
            device_id={"var": prev}, device_id_type=MESH,
        )

    def across(sweep, rows):
        near, rest = eff_hi[sweep, TILE : 2 * TILE], eff_lo[sweep, TILE : 2 * TILE]
        high, low = cross_hi[rows], cross_lo[rows]
        return dot(high, near) + (dot(high, rest) + dot(low, near))

    @pl.when(has_prev)
    def _():
        for half in halves:
            rows = piece_rows(0, half)
            take_part(tiles + half)
            crossing = summed(cross_at + half * HALF, HALF) * (1.0 / LD_SCALE)
            cross_hi[rows], cross_lo[rows] = split(crossing)
            term = across(0, rows)
            first_term[rows] = term
            back_code[0, rows] = encode(term)
            back_copy(0, half).start()
            put(0, 0, crossing.T, half * HALF)
        early_copy(0).wait_recv()
        place(0, 0, decode(early_got[0]))

    @pl.when(jnp.logical_not(has_prev))
    def _():
        put(0, 0, jnp.zeros((TILE, TILE), F32))
        for sweep in range(SWEEPS):
            place(sweep, 0, jnp.zeros((TILE, limit.shape[1]), F32))

    place(1, 1, finish(0, near_first + applied(0, 0, 0, 1)))

    @pl.when(has_prev)
    def _():
        for piece in range(BACK_LAST):
            rows = piece_rows(1, piece)
            back_code[1, rows] = encode_wide(across(1, rows))
            back_copy(1, piece).start()
        early_copy(2).wait_recv()
        early_copy(1).wait_recv()
        scale = keep_of(tail_got[pl.ds(0, 1), :])
        value = decode(early_got[1]) - (1.0 - shrinkage) * (first_term[...] * scale)
        place(1, 0, soften(value, scale))

    for t in range(last - 1):
        out[t * TILE : (t + 1) * TILE] = finish(t, applied(1, t, 0, 3))
    inner = applied(1, last - 1, 0, 2)
    edge = applied(1, last, 0, 1)

    @pl.when(jnp.logical_not(has_next))
    def _():
        back_got[...] = jnp.zeros_like(back_got)

    for piece in range(BACK_FIRST):
        rows = piece_rows(0, piece)

        @pl.when(has_next)
        def _():
            back_copy(0, piece).wait_recv()

        place(1, tiles, finish(last, near_last[rows] + decode(back_got[0, rows]), rows), rows.start)

    out[(last - 1) * TILE : last * TILE] = finish(last - 1, inner + applied(1, last - 1, 2, 1))
    edge = edge + applied(1, last, 1, 1)
    for piece in range(BACK_LAST):
        rows = piece_rows(1, piece)

        @pl.when(has_next)
        def _():
            back_copy(1, piece).wait_recv()

        combined = edge[rows] + decode_wide(back_got[1, rows])
        out[last * TILE + rows.start : last * TILE + rows.stop] = finish(last, combined, rows)

    for k in range(len(peers)):
        for message in list(range(tiles)) + [diag_message]:
            part_copy(k, message).wait_send()

    @pl.when(has_prev)
    def _():
        for k in range(len(peers)):
            for half in halves:
                part_copy(k, tiles + half).wait_send()
        for sweep, piece in places:
            back_copy(sweep, piece).wait_send()

    @pl.when(has_next)
    def _():
        for half, chunk in chunks:
            geno_copy(half, chunk).wait_send()
        for k in range(len(early)):
            early_copy(k).wait_send()


def local(genotypes, marginal, start_effects, thresholds):
    samples, variants = genotypes.shape
    traits = marginal.shape[1]
    tiles = variants // TILE
    var_size, samp_size = lax.axis_size("var"), lax.axis_size("samp")
    others = samp_size - 1
    rows = tiles * (HALF + TILE)
    dma = pltpu.SemaphoreType.DMA
    body = functools.partial(
        kernel, tiles, var_size, samp_size, 1.0 / (samples * samp_size)
    )
    return pl.pallas_call(
        body,
        out_shape=jax.ShapeDtypeStruct((variants, traits), F32),
        in_specs=[pl.BlockSpec(memory_space=pltpu.HBM)] * 4,
        out_specs=pl.BlockSpec(memory_space=pltpu.VMEM),
        scratch_shapes=[
            pltpu.VMEM((samples, variants), BF16),
            pltpu.VMEM((samples, TILE), BF16),
            pltpu.VMEM((variants, traits), F32),
            pltpu.VMEM((variants, traits), F32),
            pltpu.VMEM((1, traits), F32),
            pltpu.VMEM((rows, TILE), F32),
            pltpu.VMEM((rows, TILE), BF16),
            pltpu.VMEM((others, rows, TILE), BF16),
            pltpu.VMEM((8, TILE), F32),
            pltpu.VMEM((others, 8, TILE), F32),
            pltpu.VMEM((tiles, TILE, 3 * TILE), BF16),
            pltpu.VMEM((tiles, TILE, 3 * TILE), BF16),
            pltpu.VMEM((SWEEPS, (tiles + 1) * TILE, traits), BF16),
            pltpu.VMEM((SWEEPS, (tiles + 1) * TILE, traits), BF16),
            pltpu.VMEM((TILE, TILE), BF16),
            pltpu.VMEM((TILE, TILE), BF16),
            pltpu.VMEM((TILE, traits), F32),
            pltpu.VMEM((2, TILE, traits), BF16),
            pltpu.VMEM((2, TILE, traits), BF16),
            pltpu.VMEM((8, TILE), F32),
            pltpu.VMEM((8, TILE), F32),
            pltpu.VMEM((SWEEPS, TILE, traits), BF16),
            pltpu.VMEM((SWEEPS, TILE, traits), BF16),
            dma((tiles + 3,)),
            dma((2, CHUNKS)),
            dma((2, CHUNKS)),
            dma((others, tiles + 3)),
            dma((others, tiles + 3)),
            dma((3,)),
            dma((3,)),
            dma((SWEEPS, BACK_LAST)),
            dma((SWEEPS, BACK_LAST)),
        ],
        compiler_params=pltpu.CompilerParams(
            collective_id=0, has_side_effects=True, vmem_limit_bytes=VMEM_BYTES
        ),
    )(*(
        pltpu.with_memory_space_constraint(array, pltpu.HBM)
        for array in (genotypes, marginal, start_effects, thresholds[None, :])
    ))


def solution(mesh):
    in_specs = (P("samp", "var"), P("var", "samp"), P("var", "samp"), P("samp"))
    out_specs = P("var", "samp")
    return jax.shard_map(local, mesh=mesh, in_specs=in_specs, out_specs=out_specs, check_vma=False)
```

time: 32.7 us -> 32.9 us (level)
  the two profiles are of different devices: /device:TPU:4 before, /device:TPU:1 now
where the time goes in v1:
time: 32.9 us; the launch traced here: 32.7 us
  Pallas kernels  31.6 us (96%)
  local copies, waits for them, and re-layouts  1.15 us (3%)
    pallas_call x1, Pallas kernels, local(): pl.pallas_call(body, out_shape=jax.ShapeDtypeStruct((variants, traits), F...  31.6 us
    unnamed x1, local copies, waits for them, and re-layouts  1.15 us

profile of v1, /device:TPU:1, one launch (start us, length us, event | category | flops | bytes accessed | tf_op | source)
XLA Modules:
  0.0 32.7 jit_solution(16728023371720568468)
XLA Ops:
  0.0 31.6 %shard_map.46 = f32[768,512]{1,0:T(8,128)S(1)} custom-call(bf16[2048,768]{1,0:T(8,128)(2,1)} %geno_hbm.1, f32[768,512]{1,0:T(8,128)} %marg_hbm.1, f32[768,512]{1,0:T(8,128)} %start_hbm.1, f32[1,512]{1,0:T(1,128)} %bitcast.1), custom_call_target="tpu_custom_call" | custom-call | tf_op jit(solution)/shard_map/pallas_call | solution.py:433
  31.6 1.1 %copy.6 = f32[768,512]{1,0:T(8,128)} copy(f32[768,512]{1,0:T(8,128)S(1)} %shard_map.46) | data formatting | bytes 3145728

commit v2 on v1

--- a/solution.py
+++ b/solution.py
@@ -255,27 +255,31 @@
             put(t, 2, beside)
             put(t + 1, 0, beside.T)
 
-    def cross_step(now):
+    def cross_step(half, now):
         @pl.when(jnp.logical_and(has_prev, now))
         def _():
-            for half in halves:
-                crossing = jnp.zeros((HALF, TILE), F32)
-                for chunk in range(CHUNKS):
-                    rows = slice(chunk * depth, (chunk + 1) * depth)
-                    geno_copy(half, chunk).wait_recv()
-                    crossing = crossing + gram(
-                        halo[rows, half * HALF : (half + 1) * HALF], geno[rows, :TILE]
-                    )
-                crossing = crossing * (inv_total * LD_SCALE)
-                begin = cross_at + half * HALF
-                own[begin : begin + HALF] = crossing
-                code[begin : begin + HALF] = encode(crossing)
-                send_part(tiles + half)
+            crossing = jnp.zeros((HALF, TILE), F32)
+            for chunk in range(CHUNKS):
+                rows = slice(chunk * depth, (chunk + 1) * depth)
+                geno_copy(half, chunk).wait_recv()
+                crossing = crossing + gram(
+                    halo[rows, half * HALF : (half + 1) * HALF], geno[rows, :TILE]
+                )
+            crossing = crossing * (inv_total * LD_SCALE)
+            begin = cross_at + half * HALF
+            own[begin : begin + HALF] = crossing
+            code[begin : begin + HALF] = encode(crossing)
+            send_part(tiles + half)
 
     nearby = lax.rem(var, 2) == 1
-    cross_step(nearby)
-    for t in range(tiles):
+    far = jnp.logical_not(nearby)
+    for half in halves:
+        cross_step(half, nearby)
+    add_tile(0)
+    cross_step(0, far)
+    for t in range(1, tiles):
         add_tile(t)
+    cross_step(1, far)
     take_part(diag_message)
 
     def keep_of(whole):
@@ -308,11 +312,6 @@
     send_early(2)
     send_early(1)
     near_first = applied(0, 0, 1, 2)
-    for t in range(1, last):
-        place(1, t + 1, finish(t, applied(0, t, 0, 3)))
-
-    cross_step(jnp.logical_not(nearby))
-
     sizes = (BACK_FIRST, BACK_LAST)
     places = [(sweep, piece) for sweep in range(SWEEPS) for piece in range(sizes[sweep])]
 
@@ -336,6 +335,8 @@
 
     @pl.when(has_prev)
     def _():
+        early_copy(0).wait_recv()
+        place(0, 0, decode(early_got[0]))
         for half in halves:
             rows = piece_rows(0, half)
             take_part(tiles + half)
@@ -346,8 +347,6 @@
             back_code[0, rows] = encode(term)
             back_copy(0, half).start()
             put(0, 0, crossing.T, half * HALF)
-        early_copy(0).wait_recv()
-        place(0, 0, decode(early_got[0]))
 
     @pl.when(jnp.logical_not(has_prev))
     def _():
@@ -369,6 +368,8 @@
         value = decode(early_got[1]) - (1.0 - shrinkage) * (first_term[...] * scale)
         place(1, 0, soften(value, scale))
 
+    for t in range(1, last):
+        place(1, t + 1, finish(t, applied(0, t, 0, 3)))
     for t in range(last - 1):
         out[t * TILE : (t + 1) * TILE] = finish(t, applied(1, t, 0, 3))
     inner = applied(1, last - 1, 0, 2)
@@ -389,15 +390,6 @@
 
     out[(last - 1) * TILE : last * TILE] = finish(last - 1, inner + applied(1, last - 1, 2, 1))
     edge = edge + applied(1, last, 1, 1)
-    for piece in range(BACK_LAST):
-        rows = piece_rows(1, piece)
-
-        @pl.when(has_next)
-        def _():
-            back_copy(1, piece).wait_recv()
-
-        combined = edge[rows] + decode_wide(back_got[1, rows])
-        out[last * TILE + rows.start : last * TILE + rows.stop] = finish(last, combined, rows)
 
     for k in range(len(peers)):
         for message in list(range(tiles)) + [diag_message]:
@@ -417,6 +409,16 @@
             geno_copy(half, chunk).wait_send()
         for k in range(len(early)):
             early_copy(k).wait_send()
+
+    for piece in range(BACK_LAST):
+        rows = piece_rows(1, piece)
+
+        @pl.when(has_next)
+        def _():
+            back_copy(1, piece).wait_recv()
+
+        combined = edge[rows] + decode_wide(back_got[1, rows])
+        out[last * TILE + rows.start : last * TILE + rows.stop] = finish(last, combined, rows)
 
 
 def local(genotypes, marginal, start_effects, thresholds):

time: 32.9 us -> 29.7 us (0.903)
  Pallas kernels: 31.6 us -> 28.4 us
    pallas_call x1, Pallas kernels: 31.6 us -> 28.4 us  [local(): pl.pallas_call(body, out_shape=jax.ShapeDtypeStruct((variants, traits), F...]
where the time goes in v2:
time: 29.7 us; the launch traced here: 29.6 us
  Pallas kernels  28.4 us (96%)
  local copies, waits for them, and re-layouts  1.15 us (4%)
    pallas_call x1, Pallas kernels, local(): pl.pallas_call(body, out_shape=jax.ShapeDtypeStruct((variants, traits), F...  28.4 us
    unnamed x1, local copies, waits for them, and re-layouts  1.15 us

profile of v2, /device:TPU:1, one launch (start us, length us, event | category | flops | bytes accessed | tf_op | source)
XLA Modules:
  0.0 29.6 jit_solution(537050005274581836)
XLA Ops:
  0.0 28.4 %shard_map.46 = f32[768,512]{1,0:T(8,128)S(1)} custom-call(bf16[2048,768]{1,0:T(8,128)(2,1)} %geno_hbm.1, f32[768,512]{1,0:T(8,128)} %marg_hbm.1, f32[768,512]{1,0:T(8,128)} %start_hbm.1, f32[1,512]{1,0:T(1,128)} %bitcast.1), custom_call_target="tpu_custom_call" | custom-call | tf_op jit(solution)/shard_map/pallas_call | solution.py:435
  28.4 1.1 %copy.6 = f32[768,512]{1,0:T(8,128)} copy(f32[768,512]{1,0:T(8,128)S(1)} %shard_map.46) | data formatting | bytes 3145728

commit v3 on v2

--- a/solution.py
+++ b/solution.py
@@ -87,7 +87,7 @@
     geno_hbm, marg_hbm, start_hbm, limit_hbm, out,
     geno, halo, marg, start, limit_row, own, code, got, diag, diag_got,
     band_hi, band_lo, eff_hi, eff_lo, cross_hi, cross_lo, first_term,
-    early_code, early_got, tail_diag, tail_got, back_code, back_got,
+    early_code, early_got, tail_diag, tail_got, back_code, back_got, near,
     load_sem, geno_send, geno_recv, part_send, part_recv,
     early_send, early_recv, back_send, back_recv,
 ):
@@ -96,6 +96,12 @@
     has_prev = var > 0
     has_next = var < var_size - 1
     prev, following = var - 1, var + 1
+    nearby = lax.rem(var, 2) == 1
+    far = jnp.logical_not(nearby)
+
+    def both(*terms):
+        return functools.reduce(jnp.logical_and, terms)
+
     peers = [lax.rem(samp + k, samp_size) for k in range(1, samp_size)]
     last = tiles - 1
     tail = slice(last * TILE, tiles * TILE)
@@ -127,6 +133,7 @@
 
     for peer in peers:
         pl.semaphore_signal(barrier, inc=1, device_id={"samp": peer}, device_id_type=MESH)
+
     pl.semaphore_wait(
         barrier, len(peers) + has_prev.astype(jnp.int32) + has_next.astype(jnp.int32)
     )
@@ -193,9 +200,13 @@
             beside = product[:, TILE:]
             own[begin + HALF : begin + step] = beside
             code[begin + HALF : begin + step] = encode(beside)
-        if t == last:
-            send_part(diag_message)
-        send_part(t)
+        if t < last:
+            pl.when(far if t == 0 else var >= 0)(functools.partial(send_part, t))
+
+    @pl.when(nearby)
+    def _():
+        for message in (last, diag_message, 0):
+            send_part(message)
 
     for copy in loads[tiles:]:
         copy.wait()
@@ -275,11 +286,52 @@
     far = jnp.logical_not(nearby)
     for half in halves:
         cross_step(half, nearby)
-    add_tile(0)
+    pl.when(far)(functools.partial(add_tile, 0))
     cross_step(0, far)
-    for t in range(1, tiles):
-        add_tile(t)
+
+    @pl.when(far)
+    def _():
+        for message in (last, diag_message):
+            send_part(message)
+
+    sizes = (BACK_FIRST, BACK_LAST)
+    places = [(sweep, piece) for sweep in range(SWEEPS) for piece in range(sizes[sweep])]
+
+    def piece_rows(sweep, piece):
+        size = TILE // sizes[sweep]
+        return slice(piece * size, (piece + 1) * size)
+
+    def back_copy(sweep, piece):
+        rows = piece_rows(sweep, piece)
+        return pltpu.make_async_remote_copy(
+            src_ref=back_code.at[sweep, pl.ds(rows.start, rows.stop - rows.start)],
+            dst_ref=back_got.at[sweep, pl.ds(rows.start, rows.stop - rows.start)],
+            send_sem=back_send.at[sweep, piece], recv_sem=back_recv.at[sweep, piece],
+            device_id={"var": prev}, device_id_type=MESH,
+        )
+
+    def across(sweep, rows):
+        near, rest = eff_hi[sweep, TILE : 2 * TILE], eff_lo[sweep, TILE : 2 * TILE]
+        high, low = cross_hi[rows], cross_lo[rows]
+        return dot(high, near) + (dot(high, rest) + dot(low, near))
+
+    def first_back(half):
+        rows = piece_rows(0, half)
+        take_part(tiles + half)
+        crossing = summed(cross_at + half * HALF, HALF) * (1.0 / LD_SCALE)
+        cross_hi[rows], cross_lo[rows] = split(crossing)
+        term = across(0, rows)
+        first_term[rows] = term
+        back_code[0, rows] = encode(term)
+        back_copy(0, half).start()
+        put(0, 0, crossing.T, half * HALF)
+
     cross_step(1, far)
+
+    @pl.when(both(has_prev, far))
+    def _():
+        first_back(0)
+
     take_part(diag_message)
 
     def keep_of(whole):
@@ -294,6 +346,7 @@
         keep.append(keep_of(whole))
         if t == last:
             tail_diag[...] = jnp.broadcast_to(whole, tail_diag.shape)
+    send_early(2)
     limit = limit_row[...]
 
     def adjust(tile, combined, rows=slice(0, TILE)):
@@ -307,46 +360,23 @@
     def finish(tile, combined, rows=slice(0, TILE)):
         return soften(adjust(tile, combined, rows), keep[tile][rows])
 
-    near_last = applied(0, last, 0, 2)
-    early_code[1] = encode(adjust(last, near_last))
-    send_early(2)
+    for t in range(last, 0, -1):
+        add_tile(t)
+    near[1] = applied(0, last, 0, 2)
+    early_code[1] = encode(adjust(last, near[1]))
     send_early(1)
-    near_first = applied(0, 0, 1, 2)
-    sizes = (BACK_FIRST, BACK_LAST)
-    places = [(sweep, piece) for sweep in range(SWEEPS) for piece in range(sizes[sweep])]
-
-    def piece_rows(sweep, piece):
-        size = TILE // sizes[sweep]
-        return slice(piece * size, (piece + 1) * size)
-
-    def back_copy(sweep, piece):
-        rows = piece_rows(sweep, piece)
-        return pltpu.make_async_remote_copy(
-            src_ref=back_code.at[sweep, pl.ds(rows.start, rows.stop - rows.start)],
-            dst_ref=back_got.at[sweep, pl.ds(rows.start, rows.stop - rows.start)],
-            send_sem=back_send.at[sweep, piece], recv_sem=back_recv.at[sweep, piece],
-            device_id={"var": prev}, device_id_type=MESH,
-        )
-
-    def across(sweep, rows):
-        near, rest = eff_hi[sweep, TILE : 2 * TILE], eff_lo[sweep, TILE : 2 * TILE]
-        high, low = cross_hi[rows], cross_lo[rows]
-        return dot(high, near) + (dot(high, rest) + dot(low, near))
+    pl.when(nearby)(functools.partial(add_tile, 0))
+    near[0] = applied(0, 0, 1, 2)
+
+    @pl.when(both(has_prev, nearby))
+    def _():
+        first_back(0)
 
     @pl.when(has_prev)
     def _():
+        first_back(1)
         early_copy(0).wait_recv()
         place(0, 0, decode(early_got[0]))
-        for half in halves:
-            rows = piece_rows(0, half)
-            take_part(tiles + half)
-            crossing = summed(cross_at + half * HALF, HALF) * (1.0 / LD_SCALE)
-            cross_hi[rows], cross_lo[rows] = split(crossing)
-            term = across(0, rows)
-            first_term[rows] = term
-            back_code[0, rows] = encode(term)
-            back_copy(0, half).start()
-            put(0, 0, crossing.T, half * HALF)
 
     @pl.when(jnp.logical_not(has_prev))
     def _():
@@ -354,7 +384,7 @@
         for sweep in range(SWEEPS):
             place(sweep, 0, jnp.zeros((TILE, limit.shape[1]), F32))
 
-    place(1, 1, finish(0, near_first + applied(0, 0, 0, 1)))
+    place(1, 1, finish(0, near[0] + applied(0, 0, 0, 1)))
 
     @pl.when(has_prev)
     def _():
@@ -362,38 +392,63 @@
             rows = piece_rows(1, piece)
             back_code[1, rows] = encode_wide(across(1, rows))
             back_copy(1, piece).start()
+
+    for t in range(1, last):
+        place(1, t + 1, finish(t, applied(0, t, 0, 3)))
+
+    near[0] = applied(1, 0, 1, 2)
+    for t in range(1, last - 1):
+        out[t * TILE : (t + 1) * TILE] = finish(t, applied(1, t, 0, 3))
+    inner = applied(1, last - 1, 0, 2)
+    edge = applied(1, last, 0, 1)
+
+    @pl.when(jnp.logical_not(has_next))
+    def _():
+        back_got[...] = jnp.zeros_like(back_got)
+
+    for piece in range(BACK_FIRST):
+        rows = piece_rows(0, piece)
+
+        @pl.when(has_next)
+        def _():
+            back_copy(0, piece).wait_recv()
+
+        place(1, tiles, finish(last, near[1, rows] + decode(back_got[0, rows]), rows), rows.start)
+
+    out[(last - 1) * TILE : last * TILE] = finish(last - 1, inner + applied(1, last - 1, 2, 1))
+    edge = edge + applied(1, last, 1, 1)
+
+    @pl.when(has_prev)
+    def _():
         early_copy(2).wait_recv()
         early_copy(1).wait_recv()
         scale = keep_of(tail_got[pl.ds(0, 1), :])
         value = decode(early_got[1]) - (1.0 - shrinkage) * (first_term[...] * scale)
         place(1, 0, soften(value, scale))
 
-    for t in range(1, last):
-        place(1, t + 1, finish(t, applied(0, t, 0, 3)))
-    for t in range(last - 1):
-        out[t * TILE : (t + 1) * TILE] = finish(t, applied(1, t, 0, 3))
-    inner = applied(1, last - 1, 0, 2)
-    edge = applied(1, last, 0, 1)
-
-    @pl.when(jnp.logical_not(has_next))
-    def _():
-        back_got[...] = jnp.zeros_like(back_got)
-
-    for piece in range(BACK_FIRST):
-        rows = piece_rows(0, piece)
-
-        @pl.when(has_next)
-        def _():
-            back_copy(0, piece).wait_recv()
-
-        place(1, tiles, finish(last, near_last[rows] + decode(back_got[0, rows]), rows), rows.start)
-
-    out[(last - 1) * TILE : last * TILE] = finish(last - 1, inner + applied(1, last - 1, 2, 1))
-    edge = edge + applied(1, last, 1, 1)
+    out[:TILE] = finish(0, near[0] + applied(1, 0, 0, 1))
 
     for k in range(len(peers)):
         for message in list(range(tiles)) + [diag_message]:
             part_copy(k, message).wait_send()
+
+    @pl.when(has_next)
+    def _():
+        for half, chunk in chunks:
+            geno_copy(half, chunk).wait_send()
+        for k in range(len(early)):
+            early_copy(k).wait_send()
+
+    for piece in range(BACK_LAST):
+        rows = piece_rows(1, piece)
+
+        @pl.when(has_next)
+        def _():
+            back_copy(1, piece).wait_recv()
+
+        combined = edge[rows] + decode_wide(back_got[1, rows])
+        out[last * TILE + rows.start : last * TILE + rows.stop] = finish(last, combined, rows)
+
 
     @pl.when(has_prev)
     def _():
@@ -402,23 +457,6 @@
                 part_copy(k, tiles + half).wait_send()
         for sweep, piece in places:
             back_copy(sweep, piece).wait_send()
-
-    @pl.when(has_next)
-    def _():
-        for half, chunk in chunks:
-            geno_copy(half, chunk).wait_send()
-        for k in range(len(early)):
-            early_copy(k).wait_send()
-
-    for piece in range(BACK_LAST):
-        rows = piece_rows(1, piece)
-
-        @pl.when(has_next)
-        def _():
-            back_copy(1, piece).wait_recv()
-
-        combined = edge[rows] + decode_wide(back_got[1, rows])
-        out[last * TILE + rows.start : last * TILE + rows.stop] = finish(last, combined, rows)
 
 
 def local(genotypes, marginal, start_effects, thresholds):
@@ -461,6 +499,7 @@
             pltpu.VMEM((8, TILE), F32),
             pltpu.VMEM((SWEEPS, TILE, traits), BF16),
             pltpu.VMEM((SWEEPS, TILE, traits), BF16),
+            pltpu.VMEM((2, TILE, traits), F32),
             dma((tiles + 3,)),
             dma((2, CHUNKS)),
             dma((2, CHUNKS)),

time: 29.7 us -> 28.9 us (0.973)
  Pallas kernels: 28.4 us -> 27.6 us
    pallas_call x1, Pallas kernels: 28.4 us -> 27.6 us  [local(): pl.pallas_call(body, out_shape=jax.ShapeDtypeStruct((variants, traits), F...]
where the time goes in v3:
time: 28.9 us; the launch traced here: 28.8 us
  Pallas kernels  27.6 us (96%)
  local copies, waits for them, and re-layouts  1.15 us (4%)
    pallas_call x1, Pallas kernels, local(): pl.pallas_call(body, out_shape=jax.ShapeDtypeStruct((variants, traits), F...  27.6 us
    unnamed x1, local copies, waits for them, and re-layouts  1.15 us

profile of v3, /device:TPU:1, one launch (start us, length us, event | category | flops | bytes accessed | tf_op | source)
XLA Modules:
  0.0 28.8 jit_solution(11428590300222666471)
XLA Ops:
  0.0 27.6 %shard_map.46 = f32[768,512]{1,0:T(8,128)S(1)} custom-call(bf16[2048,768]{1,0:T(8,128)(2,1)} %geno_hbm.1, f32[768,512]{1,0:T(8,128)} %marg_hbm.1, f32[768,512]{1,0:T(8,128)} %start_hbm.1, f32[1,512]{1,0:T(1,128)} %bitcast.1), custom_call_target="tpu_custom_call" | custom-call | tf_op jit(solution)/shard_map/pallas_call | solution.py:473
  27.6 1.1 %copy.6 = f32[768,512]{1,0:T(8,128)} copy(f32[768,512]{1,0:T(8,128)S(1)} %shard_map.46) | data formatting | bytes 3145728

commit v4 on v3

--- a/solution.py
+++ b/solution.py
@@ -10,9 +10,7 @@
 TILE = 256
 HALF = TILE // 2
 SWEEPS = 2
-CHUNKS = 4
-BACK_FIRST = 2
-BACK_LAST = 4
+QUARTER = TILE // 4
 TINY = 2.0**-126
 VMEM_BYTES = 40 * 1024 * 1024
 LD_SCALE = 1024.0
@@ -85,7 +83,7 @@
 def kernel(
     tiles, var_size, samp_size, inv_total,
     geno_hbm, marg_hbm, start_hbm, limit_hbm, out,
-    geno, halo, marg, start, limit_row, own, code, got, diag, diag_got,
+    geno, halo, table, limit_row, own, code, got, diag, diag_got,
     band_hi, band_lo, eff_hi, eff_lo, cross_hi, cross_lo, first_term,
     early_code, early_got, tail_diag, tail_got, back_code, back_got, near,
     load_sem, geno_send, geno_recv, part_send, part_recv,
@@ -108,67 +106,90 @@
 
     step = HALF + TILE
     cross_at = tiles * step - TILE
+    total_rows = cross_at + TILE
     halves = range(2)
-    diag_message = tiles + 2
-
-    loads = []
-    for t in range(tiles):
-        cols = pl.ds(t * TILE, TILE)
-        loads.append(pltpu.make_async_copy(geno_hbm.at[:, cols], geno.at[:, cols], load_sem.at[t]))
-    loads.append(pltpu.make_async_copy(start_hbm, start, load_sem.at[tiles]))
-    loads.append(pltpu.make_async_copy(marg_hbm, marg, load_sem.at[tiles + 1]))
-    loads.append(pltpu.make_async_copy(limit_hbm, limit_row, load_sem.at[tiles + 2]))
+    cross_spans = [(0, HALF), (HALF, HALF)]
+    diag_message = tiles + len(cross_spans)
+    marg, start = table.at[0], table.at[1]
+    first_cols = pl.ds(0, 2 * TILE)
+    other_cols = pl.ds(2 * TILE, (tiles - 2) * TILE)
+    loads = [
+        pltpu.make_async_copy(geno_hbm.at[:, first_cols], geno.at[:, first_cols], load_sem.at[0]),
+        pltpu.make_async_copy(geno_hbm.at[:, other_cols], geno.at[:, other_cols], load_sem.at[1]),
+        pltpu.make_async_copy(start_hbm, start, load_sem.at[2]),
+        pltpu.make_async_copy(marg_hbm, marg, load_sem.at[2]),
+        pltpu.make_async_copy(limit_hbm, limit_row, load_sem.at[3]),
+    ]
+
+    barrier = pltpu.get_barrier_semaphore()
+
+    @pl.when(has_prev)
+    def _():
+        pl.semaphore_signal(barrier, inc=1, device_id={"var": prev}, device_id_type=MESH)
+
+    @pl.when(has_next)
+    def _():
+        pl.semaphore_signal(barrier, inc=1, device_id={"var": following}, device_id_type=MESH)
+
+    for peer in peers:
+        pl.semaphore_signal(barrier, inc=1, device_id={"samp": peer}, device_id_type=MESH)
+
     for copy in loads:
         copy.start()
-
-    barrier = pltpu.get_barrier_semaphore()
-
-    @pl.when(has_prev)
-    def _():
-        pl.semaphore_signal(barrier, inc=1, device_id={"var": prev}, device_id_type=MESH)
-
-    @pl.when(has_next)
-    def _():
-        pl.semaphore_signal(barrier, inc=1, device_id={"var": following}, device_id_type=MESH)
-
-    for peer in peers:
-        pl.semaphore_signal(barrier, inc=1, device_id={"samp": peer}, device_id_type=MESH)
 
     pl.semaphore_wait(
         barrier, len(peers) + has_prev.astype(jnp.int32) + has_next.astype(jnp.int32)
     )
 
-    depth = geno.shape[0] // CHUNKS
-    chunks = [(half, chunk) for half in halves for chunk in range(CHUNKS)]
-
-    def geno_copy(half, chunk):
-        rows = pl.ds(chunk * depth, depth)
+    depth = geno.shape[0]
+    cut = depth - depth // 4
+    geno_spans = [(0, 0, depth), (1, 0, cut), (1, cut, depth)]
+
+    def geno_copy(index):
+        half, begin, end = geno_spans[index]
+        rows = pl.ds(begin, end - begin)
         return pltpu.make_async_remote_copy(
             src_ref=geno_hbm.at[rows, pl.ds(last * TILE + half * HALF, HALF)],
             dst_ref=halo.at[rows, pl.ds(half * HALF, HALF)],
-            send_sem=geno_send.at[half, chunk], recv_sem=geno_recv.at[half, chunk],
+            send_sem=geno_send, recv_sem=geno_recv.at[index],
             device_id={"var": following}, device_id_type=MESH,
         )
 
+    def geno_sent():
+        return pltpu.make_async_remote_copy(
+            src_ref=geno_hbm.at[:, pl.ds(last * TILE, TILE)], dst_ref=halo,
+            send_sem=geno_send, recv_sem=geno_recv.at[0],
+            device_id={"var": following}, device_id_type=MESH,
+        )
+
     @pl.when(has_next)
     def _():
-        for half, chunk in chunks:
-            geno_copy(half, chunk).start()
+        for index in range(len(geno_spans)):
+            geno_copy(index).start()
+
+    def code_copy(k, begin, end, arrival):
+        rows = pl.ds(begin, end - begin)
+        return pltpu.make_async_remote_copy(
+            src_ref=code.at[rows], dst_ref=got.at[k, rows],
+            send_sem=part_send.at[k, 0], recv_sem=part_recv.at[k, arrival],
+            device_id={"samp": peers[k]}, device_id_type=MESH,
+        )
+
+    def diag_copy(k):
+        return pltpu.make_async_remote_copy(
+            src_ref=diag, dst_ref=diag_got.at[k],
+            send_sem=part_send.at[k, 1], recv_sem=part_recv.at[k, 2 + len(cross_spans)],
+            device_id={"samp": peers[k]}, device_id_type=MESH,
+        )
 
     def part_copy(k, message):
         if message == diag_message:
-            src, dst = diag, diag_got.at[k]
-        else:
-            if message < tiles:
-                rows = pl.ds(message * step, HALF if message == last else step)
-            else:
-                rows = pl.ds(cross_at + (message - tiles) * HALF, HALF)
-            src, dst = code.at[rows], got.at[k, rows]
-        return pltpu.make_async_remote_copy(
-            src_ref=src, dst_ref=dst,
-            send_sem=part_send.at[k, message], recv_sem=part_recv.at[k, message],
-            device_id={"samp": peers[k]}, device_id_type=MESH,
-        )
+            return diag_copy(k)
+        if message < tiles:
+            begin = message * step
+            return code_copy(k, begin, min(begin + step, cross_at), min(message, 1))
+        first, size = cross_spans[message - tiles]
+        return code_copy(k, cross_at + first, cross_at + first + size, 2 + message - tiles)
 
     def send_part(message):
         for k in range(len(peers)):
@@ -176,17 +197,18 @@
 
     def take_part(message):
         for k in range(len(peers)):
-            part_copy(k, message).wait_recv()
+            if 0 < message < tiles:
+                code_copy(k, step, cross_at, 1).wait_recv()
+            else:
+                part_copy(k, message).wait_recv()
 
     diag[...] = jnp.zeros_like(diag)
     row, col = iota_pair(TILE)
     on_diagonal = row == col
 
     for t in range(tiles):
-        if t == 0:
-            loads[0].wait()
-        if t + 1 < tiles:
-            loads[t + 1].wait()
+        if t < 2:
+            loads[t].wait()
         reach = min(t + 2, tiles) * TILE
         product = gram(geno[:, t * TILE : (t + 1) * TILE], geno[:, t * TILE : reach])
         product = product * (inv_total * LD_SCALE)
@@ -208,8 +230,8 @@
         for message in (last, diag_message, 0):
             send_part(message)
 
-    for copy in loads[tiles:]:
-        copy.wait()
+    pltpu.make_async_copy(table, table, load_sem.at[2]).wait()
+    loads[4].wait()
 
     def place(sweep, slot, value, first=0):
         begin = slot * TILE + first
@@ -217,12 +239,18 @@
         eff_hi[sweep, begin : begin + value.shape[0]] = high
         eff_lo[sweep, begin : begin + value.shape[0]] = low
 
-    early = [(early_code.at[k], early_got.at[k]) for k in range(2)] + [(tail_diag, tail_got)]
+    early = [(early_code.at[k], early_got.at[k], 0) for k in range(2)] + [(tail_diag, tail_got, 1)]
 
     def early_copy(k):
-        src, dst = early[k]
-        return pltpu.make_async_remote_copy(
-            src_ref=src, dst_ref=dst, send_sem=early_send.at[k], recv_sem=early_recv.at[k],
+        src, dst, departure = early[k]
+        return pltpu.make_async_remote_copy(
+            src_ref=src, dst_ref=dst, send_sem=early_send.at[departure], recv_sem=early_recv.at[k],
+            device_id={"var": following}, device_id_type=MESH,
+        )
+
+    def early_sent():
+        return pltpu.make_async_remote_copy(
+            src_ref=early_code, dst_ref=early_got, send_sem=early_send.at[0], recv_sem=early_recv.at[0],
             device_id={"var": following}, device_id_type=MESH,
         )
 
@@ -258,7 +286,6 @@
         return dot(high, near) + (dot(high, rest) + dot(low, near))
 
     def add_tile(t):
-        take_part(t)
         begin = t * step
         put(t, 1, unpack_symmetric(summed(begin, HALF)) * (1.0 / LD_SCALE))
         if t + 1 < tiles:
@@ -269,44 +296,50 @@
     def cross_step(half, now):
         @pl.when(jnp.logical_and(has_prev, now))
         def _():
-            crossing = jnp.zeros((HALF, TILE), F32)
-            for chunk in range(CHUNKS):
-                rows = slice(chunk * depth, (chunk + 1) * depth)
-                geno_copy(half, chunk).wait_recv()
-                crossing = crossing + gram(
-                    halo[rows, half * HALF : (half + 1) * HALF], geno[rows, :TILE]
-                )
-            crossing = crossing * (inv_total * LD_SCALE)
             begin = cross_at + half * HALF
-            own[begin : begin + HALF] = crossing
+            for index, (side, first, end) in enumerate(geno_spans):
+                if side == half:
+                    geno_copy(index).wait_recv()
+                    crossing = gram(
+                        halo[first:end, half * HALF : (half + 1) * HALF], geno[first:end, :TILE]
+                    )
+                    crossing = crossing * (inv_total * LD_SCALE)
+                    if first > 0:
+                        crossing = crossing + own[begin : begin + HALF]
+                    own[begin : begin + HALF] = crossing
             code[begin : begin + HALF] = encode(crossing)
-            send_part(tiles + half)
-
-    nearby = lax.rem(var, 2) == 1
-    far = jnp.logical_not(nearby)
+            for piece, (first, size) in enumerate(cross_spans):
+                if first // HALF == half:
+                    send_part(tiles + piece)
+
     for half in halves:
         cross_step(half, nearby)
-    pl.when(far)(functools.partial(add_tile, 0))
+    def start_first():
+        take_part(0)
+        add_tile(0)
+        near[0] = applied(0, 0, 1, 2)
+
     cross_step(0, far)
 
     @pl.when(far)
     def _():
         for message in (last, diag_message):
             send_part(message)
-
-    sizes = (BACK_FIRST, BACK_LAST)
-    places = [(sweep, piece) for sweep in range(SWEEPS) for piece in range(sizes[sweep])]
-
-    def piece_rows(sweep, piece):
-        size = TILE // sizes[sweep]
-        return slice(piece * size, (piece + 1) * size)
-
-    def back_copy(sweep, piece):
-        rows = piece_rows(sweep, piece)
-        return pltpu.make_async_remote_copy(
-            src_ref=back_code.at[sweep, pl.ds(rows.start, rows.stop - rows.start)],
-            dst_ref=back_got.at[sweep, pl.ds(rows.start, rows.stop - rows.start)],
-            send_sem=back_send.at[sweep, piece], recv_sem=back_recv.at[sweep, piece],
+        start_first()
+
+    back_spans = [cross_spans, [(k * QUARTER, QUARTER) for k in range(4)]]
+
+    def back_copy(sweep, first, size, arrival):
+        rows = pl.ds(first, size)
+        return pltpu.make_async_remote_copy(
+            src_ref=back_code.at[sweep, rows], dst_ref=back_got.at[sweep, rows],
+            send_sem=back_send, recv_sem=back_recv.at[arrival],
+            device_id={"var": prev}, device_id_type=MESH,
+        )
+
+    def back_sent():
+        return pltpu.make_async_remote_copy(
+            src_ref=back_code, dst_ref=back_got, send_sem=back_send, recv_sem=back_recv.at[0],
             device_id={"var": prev}, device_id_type=MESH,
         )
 
@@ -315,16 +348,17 @@
         high, low = cross_hi[rows], cross_lo[rows]
         return dot(high, near) + (dot(high, rest) + dot(low, near))
 
-    def first_back(half):
-        rows = piece_rows(0, half)
-        take_part(tiles + half)
-        crossing = summed(cross_at + half * HALF, HALF) * (1.0 / LD_SCALE)
+    def first_back(piece):
+        first, size = cross_spans[piece]
+        rows = slice(first, first + size)
+        take_part(tiles + piece)
+        crossing = summed(cross_at + first, size) * (1.0 / LD_SCALE)
         cross_hi[rows], cross_lo[rows] = split(crossing)
         term = across(0, rows)
         first_term[rows] = term
         back_code[0, rows] = encode(term)
-        back_copy(0, half).start()
-        put(0, 0, crossing.T, half * HALF)
+        back_copy(0, first, size, 0).start()
+        put(0, 0, crossing.T, first)
 
     cross_step(1, far)
 
@@ -360,13 +394,13 @@
     def finish(tile, combined, rows=slice(0, TILE)):
         return soften(adjust(tile, combined, rows), keep[tile][rows])
 
+    take_part(last)
     for t in range(last, 0, -1):
         add_tile(t)
     near[1] = applied(0, last, 0, 2)
     early_code[1] = encode(adjust(last, near[1]))
     send_early(1)
-    pl.when(nearby)(functools.partial(add_tile, 0))
-    near[0] = applied(0, 0, 1, 2)
+    pl.when(nearby)(start_first)
 
     @pl.when(both(has_prev, nearby))
     def _():
@@ -374,7 +408,8 @@
 
     @pl.when(has_prev)
     def _():
-        first_back(1)
+        for piece in range(1, len(cross_spans)):
+            first_back(piece)
         early_copy(0).wait_recv()
         place(0, 0, decode(early_got[0]))
 
@@ -388,10 +423,10 @@
 
     @pl.when(has_prev)
     def _():
-        for piece in range(BACK_LAST):
-            rows = piece_rows(1, piece)
+        for piece, (first, size) in enumerate(back_spans[1]):
+            rows = slice(first, first + size)
             back_code[1, rows] = encode_wide(across(1, rows))
-            back_copy(1, piece).start()
+            back_copy(1, first, size, 1 + piece // 3).start()
 
     for t in range(1, last):
         place(1, t + 1, finish(t, applied(0, t, 0, 3)))
@@ -406,15 +441,11 @@
     def _():
         back_got[...] = jnp.zeros_like(back_got)
 
-    for piece in range(BACK_FIRST):
-        rows = piece_rows(0, piece)
-
-        @pl.when(has_next)
-        def _():
-            back_copy(0, piece).wait_recv()
-
-        place(1, tiles, finish(last, near[1, rows] + decode(back_got[0, rows]), rows), rows.start)
-
+    @pl.when(has_next)
+    def _():
+        back_copy(0, 0, TILE, 0).wait_recv()
+
+    place(1, tiles, finish(last, near[1] + decode(back_got[0])))
     out[(last - 1) * TILE : last * TILE] = finish(last - 1, inner + applied(1, last - 1, 2, 1))
     edge = edge + applied(1, last, 1, 1)
 
@@ -429,22 +460,28 @@
     out[:TILE] = finish(0, near[0] + applied(1, 0, 0, 1))
 
     for k in range(len(peers)):
-        for message in list(range(tiles)) + [diag_message]:
-            part_copy(k, message).wait_send()
+        diag_copy(k).wait_send()
+
+        @pl.when(has_prev)
+        def _():
+            code_copy(k, 0, total_rows, 0).wait_send()
+
+        @pl.when(jnp.logical_not(has_prev))
+        def _():
+            code_copy(k, 0, cross_at, 0).wait_send()
 
     @pl.when(has_next)
     def _():
-        for half, chunk in chunks:
-            geno_copy(half, chunk).wait_send()
-        for k in range(len(early)):
-            early_copy(k).wait_send()
-
-    for piece in range(BACK_LAST):
-        rows = piece_rows(1, piece)
+        geno_sent().wait_send()
+        early_sent().wait_send()
+        early_copy(2).wait_send()
+
+    for first, size in ((0, 3 * QUARTER), (3 * QUARTER, QUARTER)):
+        rows = slice(first, first + size)
 
         @pl.when(has_next)
         def _():
-            back_copy(1, piece).wait_recv()
+            back_copy(1, first, size, 1 + first // (3 * QUARTER)).wait_recv()
 
         combined = edge[rows] + decode_wide(back_got[1, rows])
         out[last * TILE + rows.start : last * TILE + rows.stop] = finish(last, combined, rows)
@@ -452,11 +489,7 @@
 
     @pl.when(has_prev)
     def _():
-        for k in range(len(peers)):
-            for half in halves:
-                part_copy(k, tiles + half).wait_send()
-        for sweep, piece in places:
-            back_copy(sweep, piece).wait_send()
+        back_sent().wait_send()
 
 
 def local(genotypes, marginal, start_effects, thresholds):
@@ -478,8 +511,7 @@
         scratch_shapes=[
             pltpu.VMEM((samples, variants), BF16),
             pltpu.VMEM((samples, TILE), BF16),
-            pltpu.VMEM((variants, traits), F32),
-            pltpu.VMEM((variants, traits), F32),
+            pltpu.VMEM((2, variants, traits), F32),
             pltpu.VMEM((1, traits), F32),
             pltpu.VMEM((rows, TILE), F32),
             pltpu.VMEM((rows, TILE), BF16),
@@ -500,15 +532,15 @@
             pltpu.VMEM((SWEEPS, TILE, traits), BF16),
             pltpu.VMEM((SWEEPS, TILE, traits), BF16),
             pltpu.VMEM((2, TILE, traits), F32),
-            dma((tiles + 3,)),
-            dma((2, CHUNKS)),
-            dma((2, CHUNKS)),
-            dma((others, tiles + 3)),
-            dma((others, tiles + 3)),
+            dma((4,)),
+            dma,
             dma((3,)),
+            dma((others, 2)),
+            dma((others, 5)),
+            dma((2,)),
             dma((3,)),
-            dma((SWEEPS, BACK_LAST)),
-            dma((SWEEPS, BACK_LAST)),
+            dma,
+            dma((3,)),
         ],
         compiler_params=pltpu.CompilerParams(
             collective_id=0, has_side_effects=True, vmem_limit_bytes=VMEM_BYTES

time: 28.9 us -> 28.5 us (0.986)
  Pallas kernels: 27.6 us -> 27.1 us
    pallas_call x1, Pallas kernels: 27.6 us -> 27.1 us  [local(): pl.pallas_call(body, out_shape=jax.ShapeDtypeStruct((variants, traits), F...]
where the time goes in v4:
time: 28.5 us; the launch traced here: 28.3 us
  Pallas kernels  27.1 us (95%)
  local copies, waits for them, and re-layouts  1.15 us (4%)
    pallas_call x1, Pallas kernels, local(): pl.pallas_call(body, out_shape=jax.ShapeDtypeStruct((variants, traits), F...  27.1 us
    unnamed x1, local copies, waits for them, and re-layouts  1.15 us

profile of v4, /device:TPU:1, one launch (start us, length us, event | category | flops | bytes accessed | tf_op | source)
XLA Modules:
  0.0 28.3 jit_solution(17791793271481727473)
XLA Ops:
  0.0 27.1 %shard_map.46 = f32[768,512]{1,0:T(8,128)S(1)} custom-call(bf16[2048,768]{1,0:T(8,128)(2,1)} %geno_hbm.1, f32[768,512]{1,0:T(8,128)} %marg_hbm.1, f32[768,512]{1,0:T(8,128)} %start_hbm.1, f32[1,512]{1,0:T(1,128)} %bitcast.1), custom_call_target="tpu_custom_call" | custom-call | tf_op jit(solution)/shard_map/pallas_call | solution.py:506
  27.2 1.1 %copy.6 = f32[768,512]{1,0:T(8,128)} copy(f32[768,512]{1,0:T(8,128)S(1)} %shard_map.46) | data formatting | bytes 3145728

commit v5 on v4

--- a/solution.py
+++ b/solution.py
@@ -11,6 +11,7 @@
 HALF = TILE // 2
 SWEEPS = 2
 QUARTER = TILE // 4
+RELAYS = 3
 TINY = 2.0**-126
 VMEM_BYTES = 40 * 1024 * 1024
 LD_SCALE = 1024.0
@@ -85,9 +86,9 @@
     geno_hbm, marg_hbm, start_hbm, limit_hbm, out,
     geno, halo, table, limit_row, own, code, got, diag, diag_got,
     band_hi, band_lo, eff_hi, eff_lo, cross_hi, cross_lo, first_term,
-    early_code, early_got, tail_diag, tail_got, back_code, back_got, near,
+    early_code, early_got, tail_diag, tail_got, back_code, back_got, near, held,
     load_sem, geno_send, geno_recv, part_send, part_recv,
-    early_send, early_recv, back_send, back_recv,
+    early_send, early_recv, back_send, back_recv, held_send, held_recv,
 ):
     var = lax.axis_index("var")
     samp = lax.axis_index("samp")
@@ -134,16 +135,51 @@
     for peer in peers:
         pl.semaphore_signal(barrier, inc=1, device_id={"samp": peer}, device_id_type=MESH)
 
+    routes = [(4 * k + 3, 0, 4 * k + 4, k) for k in range(RELAYS)]
+    routes = [route for route in routes if max(route) < var_size]
+    waits = has_prev.astype(jnp.int32) + has_next.astype(jnp.int32)
+    relayed = var < 0
+    for sender, middle, target, _ in routes:
+        @pl.when(var == middle)
+        def _():
+            pl.semaphore_signal(barrier, inc=1, device_id={"var": sender}, device_id_type=MESH)
+
+        @pl.when(var == target)
+        def _():
+            pl.semaphore_signal(barrier, inc=1, device_id={"var": middle}, device_id_type=MESH)
+
+        waits = waits + (var == sender).astype(jnp.int32) + (var == middle).astype(jnp.int32)
+        relayed = jnp.logical_or(relayed, var == sender)
+
     for copy in loads:
         copy.start()
 
-    pl.semaphore_wait(
-        barrier, len(peers) + has_prev.astype(jnp.int32) + has_next.astype(jnp.int32)
-    )
+    pl.semaphore_wait(barrier, len(peers) + waits)
 
     depth = geno.shape[0]
     cut = depth - depth // 4
-    geno_spans = [(0, 0, depth), (1, 0, cut), (1, cut, depth)]
+    small = depth // 8
+    geno_spans = [(0, 0, depth), (1, 0, small), (1, small, cut), (1, cut, depth)]
+    piece_rows, piece_cols = pl.ds(0, small), pl.ds(last * TILE + HALF, HALF)
+
+    def outward_copy(middle, slot):
+        return pltpu.make_async_remote_copy(
+            src_ref=geno_hbm.at[piece_rows, piece_cols], dst_ref=held.at[slot],
+            send_sem=geno_send, recv_sem=held_recv.at[slot],
+            device_id={"var": middle}, device_id_type=MESH,
+        )
+
+    def onward_copy(target, slot):
+        return pltpu.make_async_remote_copy(
+            src_ref=held.at[slot], dst_ref=halo.at[piece_rows, pl.ds(HALF, HALF)],
+            send_sem=held_send.at[slot], recv_sem=geno_recv.at[1],
+            device_id={"var": target}, device_id_type=MESH,
+        )
+
+    for sender, middle, _, slot in routes:
+        @pl.when(var == sender)
+        def _():
+            outward_copy(middle, slot).start()
 
     def geno_copy(index):
         half, begin, end = geno_spans[index]
@@ -164,7 +200,15 @@
 
     @pl.when(has_next)
     def _():
-        for index in range(len(geno_spans)):
+        geno_copy(0).start()
+
+    @pl.when(both(has_next, jnp.logical_not(relayed)))
+    def _():
+        geno_copy(1).start()
+
+    @pl.when(has_next)
+    def _():
+        for index in (2, 3):
             geno_copy(index).start()
 
     def code_copy(k, begin, end, arrival):
@@ -297,16 +341,17 @@
         @pl.when(jnp.logical_and(has_prev, now))
         def _():
             begin = cross_at + half * HALF
-            for index, (side, first, end) in enumerate(geno_spans):
-                if side == half:
+            for indices in ((0,),) if half == 0 else ((1, 2), (3,)):
+                for index in indices:
                     geno_copy(index).wait_recv()
-                    crossing = gram(
-                        halo[first:end, half * HALF : (half + 1) * HALF], geno[first:end, :TILE]
-                    )
-                    crossing = crossing * (inv_total * LD_SCALE)
-                    if first > 0:
-                        crossing = crossing + own[begin : begin + HALF]
-                    own[begin : begin + HALF] = crossing
+                first, end = geno_spans[indices[0]][1], geno_spans[indices[-1]][2]
+                crossing = gram(
+                    halo[first:end, half * HALF : (half + 1) * HALF], geno[first:end, :TILE]
+                )
+                crossing = crossing * (inv_total * LD_SCALE)
+                if first > 0:
+                    crossing = crossing + own[begin : begin + HALF]
+                own[begin : begin + HALF] = crossing
             code[begin : begin + HALF] = encode(crossing)
             for piece, (first, size) in enumerate(cross_spans):
                 if first // HALF == half:
@@ -314,6 +359,12 @@
 
     for half in halves:
         cross_step(half, nearby)
+    for _, middle, target, slot in routes:
+        @pl.when(var == middle)
+        def _():
+            outward_copy(middle, slot).wait_recv()
+            onward_copy(target, slot).start()
+
     def start_first():
         take_part(0)
         add_tile(0)
@@ -449,6 +500,19 @@
     out[(last - 1) * TILE : last * TILE] = finish(last - 1, inner + applied(1, last - 1, 2, 1))
     edge = edge + applied(1, last, 1, 1)
 
+    def end_last():
+        for first, size in ((0, 3 * QUARTER), (3 * QUARTER, QUARTER)):
+            rows = slice(first, first + size)
+
+            @pl.when(has_next)
+            def _():
+                back_copy(1, first, size, 1 + first // (3 * QUARTER)).wait_recv()
+
+            combined = edge[rows] + decode_wide(back_got[1, rows])
+            out[last * TILE + rows.start : last * TILE + rows.stop] = finish(last, combined, rows)
+
+    pl.when(far)(end_last)
+
     @pl.when(has_prev)
     def _():
         early_copy(2).wait_recv()
@@ -476,16 +540,12 @@
         early_sent().wait_send()
         early_copy(2).wait_send()
 
-    for first, size in ((0, 3 * QUARTER), (3 * QUARTER, QUARTER)):
-        rows = slice(first, first + size)
-
-        @pl.when(has_next)
-        def _():
-            back_copy(1, first, size, 1 + first // (3 * QUARTER)).wait_recv()
-
-        combined = edge[rows] + decode_wide(back_got[1, rows])
-        out[last * TILE + rows.start : last * TILE + rows.stop] = finish(last, combined, rows)
-
+    for _, middle, target, slot in routes:
+        @pl.when(var == middle)
+        def _():
+            onward_copy(target, slot).wait_send()
+
+    pl.when(nearby)(end_last)
 
     @pl.when(has_prev)
     def _():
@@ -532,15 +592,18 @@
             pltpu.VMEM((SWEEPS, TILE, traits), BF16),
             pltpu.VMEM((SWEEPS, TILE, traits), BF16),
             pltpu.VMEM((2, TILE, traits), F32),
+            pltpu.VMEM((RELAYS, samples // 8, HALF), BF16),
             dma((4,)),
             dma,
-            dma((3,)),
+            dma((4,)),
             dma((others, 2)),
             dma((others, 5)),
             dma((2,)),
             dma((3,)),
             dma,
             dma((3,)),
+            dma((RELAYS,)),
+            dma((RELAYS,)),
         ],
         compiler_params=pltpu.CompilerParams(
             collective_id=0, has_side_effects=True, vmem_limit_bytes=VMEM_BYTES

time: 28.5 us -> 28.5 us (level)
  no operation moved by 1% of the time
where the time goes in v5:
time: 28.5 us; the launch traced here: 28.4 us
  Pallas kernels  27.2 us (95%)
  local copies, waits for them, and re-layouts  1.15 us (4%)
    pallas_call x1, Pallas kernels, local(): pl.pallas_call(body, out_shape=jax.ShapeDtypeStruct((variants, traits), F...  27.2 us
    unnamed x1, local copies, waits for them, and re-layouts  1.15 us

profile of v5, /device:TPU:1, one launch (start us, length us, event | category | flops | bytes accessed | tf_op | source)
XLA Modules:
  0.0 28.4 jit_solution(4686697937283774760)
XLA Ops:
  0.0 27.2 %shard_map.46 = f32[768,512]{1,0:T(8,128)S(1)} custom-call(bf16[2048,768]{1,0:T(8,128)(2,1)} %geno_hbm.1, f32[768,512]{1,0:T(8,128)} %marg_hbm.1, f32[768,512]{1,0:T(8,128)} %start_hbm.1, f32[1,512]{1,0:T(1,128)} %bitcast.1), custom_call_target="tpu_custom_call" | custom-call | tf_op jit(solution)/shard_map/pallas_call | solution.py:566
  27.2 1.1 %copy.6 = f32[768,512]{1,0:T(8,128)} copy(f32[768,512]{1,0:T(8,128)S(1)} %shard_map.46) | data formatting | bytes 3145728

commit v6 on v5

--- a/solution.py
+++ b/solution.py
@@ -87,8 +87,9 @@
     geno, halo, table, limit_row, own, code, got, diag, diag_got,
     band_hi, band_lo, eff_hi, eff_lo, cross_hi, cross_lo, first_term,
     early_code, early_got, tail_diag, tail_got, back_code, back_got, near, held,
+    extra_code, extra_got, half_code, half_got,
     load_sem, geno_send, geno_recv, part_send, part_recv,
-    early_send, early_recv, back_send, back_recv, held_send, held_recv,
+    early_send, early_recv, back_send, back_recv, held_send, held_recv, extra_send, extra_recv,
 ):
     var = lax.axis_index("var")
     samp = lax.axis_index("samp")
@@ -97,6 +98,8 @@
     prev, following = var - 1, var + 1
     nearby = lax.rem(var, 2) == 1
     far = jnp.logical_not(nearby)
+
+    leads, follows = jnp.logical_and(var == 1, has_next), var == 2
 
     def both(*terms):
         return functools.reduce(jnp.logical_and, terms)
@@ -172,7 +175,7 @@
     def onward_copy(target, slot):
         return pltpu.make_async_remote_copy(
             src_ref=held.at[slot], dst_ref=halo.at[piece_rows, pl.ds(HALF, HALF)],
-            send_sem=held_send.at[slot], recv_sem=geno_recv.at[1],
+            send_sem=held_send, recv_sem=geno_recv.at[1],
             device_id={"var": target}, device_id_type=MESH,
         )
 
@@ -277,13 +280,20 @@
     pltpu.make_async_copy(table, table, load_sem.at[2]).wait()
     loads[4].wait()
 
-    def place(sweep, slot, value, first=0):
-        begin = slot * TILE + first
+    def place(sweep, slot, value, cols=slice(None)):
+        begin = slot * TILE
         high, low = split(value)
-        eff_hi[sweep, begin : begin + value.shape[0]] = high
-        eff_lo[sweep, begin : begin + value.shape[0]] = low
-
-    early = [(early_code.at[k], early_got.at[k], 0) for k in range(2)] + [(tail_diag, tail_got, 1)]
+        eff_hi[sweep, begin : begin + TILE, cols] = high
+        eff_lo[sweep, begin : begin + TILE, cols] = low
+
+    traits = start_hbm.shape[1]
+    width = traits // 2 if traits % 256 == 0 else traits
+    sides = [slice(begin, begin + width) for begin in range(0, traits, width)]
+    full = slice(0, traits)
+    early = [(early_code.at[0], early_got.at[0], 0), (tail_diag, tail_got, 1)]
+    for side in sides:
+        cols = pl.ds(side.start, width)
+        early.append((early_code.at[1, :, cols], early_got.at[1, :, cols], 0))
 
     def early_copy(k):
         src, dst, departure = early[k]
@@ -303,8 +313,23 @@
         def _():
             early_copy(k).start()
 
+    extras = [(extra_code, extra_got), (half_code, half_got)]
+
+    def extra_copy(k):
+        src, dst = extras[k]
+        return pltpu.make_async_remote_copy(
+            src_ref=src, dst_ref=dst, send_sem=extra_send.at[k], recv_sem=extra_recv.at[k],
+            device_id={"var": prev}, device_id_type=MESH,
+        )
+
     early_code[0] = encode(start[tail])
     send_early(0)
+
+    @pl.when(follows)
+    def _():
+        extra_code[...] = encode(start[:TILE])
+        extra_copy(0).start()
+
     for t in range(tiles):
         place(0, t + 1, start[t * TILE : (t + 1) * TILE])
 
@@ -322,11 +347,11 @@
 
     dot = functools.partial(jnp.dot, preferred_element_type=F32)
 
-    def applied(sweep, tile, first, count):
+    def applied(sweep, tile, first, count, cols=slice(None)):
         across = slice(first * TILE, (first + count) * TILE)
         rows = slice((tile + first) * TILE, (tile + first + count) * TILE)
         high, low = band_hi[tile, :, across], band_lo[tile, :, across]
-        near, rest = eff_hi[sweep, rows], eff_lo[sweep, rows]
+        near, rest = eff_hi[sweep, rows, cols], eff_lo[sweep, rows, cols]
         return dot(high, near) + (dot(high, rest) + dot(low, near))
 
     def add_tile(t):
@@ -380,17 +405,11 @@
 
     back_spans = [cross_spans, [(k * QUARTER, QUARTER) for k in range(4)]]
 
-    def back_copy(sweep, first, size, arrival):
-        rows = pl.ds(first, size)
-        return pltpu.make_async_remote_copy(
-            src_ref=back_code.at[sweep, rows], dst_ref=back_got.at[sweep, rows],
+    def back_copy(begin, size, arrival):
+        rows = pl.ds(begin, size)
+        return pltpu.make_async_remote_copy(
+            src_ref=back_code.at[rows], dst_ref=back_got.at[rows],
             send_sem=back_send, recv_sem=back_recv.at[arrival],
-            device_id={"var": prev}, device_id_type=MESH,
-        )
-
-    def back_sent():
-        return pltpu.make_async_remote_copy(
-            src_ref=back_code, dst_ref=back_got, send_sem=back_send, recv_sem=back_recv.at[0],
             device_id={"var": prev}, device_id_type=MESH,
         )
 
@@ -399,16 +418,21 @@
         high, low = cross_hi[rows], cross_lo[rows]
         return dot(high, near) + (dot(high, rest) + dot(low, near))
 
-    def first_back(piece):
+    def first_back(piece, product=True):
         first, size = cross_spans[piece]
         rows = slice(first, first + size)
         take_part(tiles + piece)
-        crossing = summed(cross_at + first, size) * (1.0 / LD_SCALE)
+        scaled = summed(cross_at + first, size)
+        if not product:
+            half_code[...] = encode(scaled)
+            extra_copy(1).start()
+        crossing = scaled * (1.0 / LD_SCALE)
         cross_hi[rows], cross_lo[rows] = split(crossing)
-        term = across(0, rows)
-        first_term[rows] = term
-        back_code[0, rows] = encode(term)
-        back_copy(0, first, size, 0).start()
+        if product:
+            term = across(0, rows)
+            first_term[rows] = term
+            back_code[rows] = encode(term)
+            back_copy(first, size, 0).start()
         put(0, 0, crossing.T, first)
 
     cross_step(1, far)
@@ -431,36 +455,45 @@
         keep.append(keep_of(whole))
         if t == last:
             tail_diag[...] = jnp.broadcast_to(whole, tail_diag.shape)
-    send_early(2)
+    send_early(1)
     limit = limit_row[...]
 
-    def adjust(tile, combined, rows=slice(0, TILE)):
+    every = slice(0, TILE)
+
+    def adjust(tile, combined, rows=every, cols=full):
         shift = slice(tile * TILE + rows.start, tile * TILE + rows.stop)
-        return (marg[shift] - (1.0 - shrinkage) * combined) * keep[tile][rows]
-
-    def soften(value, scale):
-        bound = limit * scale
+        return (marg[shift, cols] - (1.0 - shrinkage) * combined) * keep[tile][rows]
+
+    def soften(value, scale, cols=full):
+        bound = limit[:, cols] * scale
         return value - jnp.clip(value, -bound, bound)
 
-    def finish(tile, combined, rows=slice(0, TILE)):
-        return soften(adjust(tile, combined, rows), keep[tile][rows])
+    def finish(tile, combined, rows=every, cols=full):
+        return soften(adjust(tile, combined, rows, cols), keep[tile][rows], cols)
 
     take_part(last)
     for t in range(last, 0, -1):
         add_tile(t)
     near[1] = applied(0, last, 0, 2)
-    early_code[1] = encode(adjust(last, near[1]))
-    send_early(1)
+    for k, side in enumerate(sides):
+        early_code[1, :, side] = encode(adjust(last, near[1, :, side], every, side))
+        send_early(2 + k)
     pl.when(nearby)(start_first)
 
     @pl.when(both(has_prev, nearby))
     def _():
         first_back(0)
 
+    @pl.when(both(has_prev, jnp.logical_not(follows)))
+    def _():
+        first_back(1)
+
+    @pl.when(follows)
+    def _():
+        first_back(1, False)
+
     @pl.when(has_prev)
     def _():
-        for piece in range(1, len(cross_spans)):
-            first_back(piece)
         early_copy(0).wait_recv()
         place(0, 0, decode(early_got[0]))
 
@@ -476,8 +509,12 @@
     def _():
         for piece, (first, size) in enumerate(back_spans[1]):
             rows = slice(first, first + size)
-            back_code[1, rows] = encode_wide(across(1, rows))
-            back_copy(1, first, size, 1 + piece // 3).start()
+            back_code[TILE + first : TILE + first + size] = encode_wide(across(1, rows))
+            back_copy(TILE + first, size, 1 + piece // 3).start()
+
+    @pl.when(follows)
+    def _():
+        first_term[HALF:] = across(0, slice(HALF, TILE))
 
     for t in range(1, last):
         place(1, t + 1, finish(t, applied(0, t, 0, 3)))
@@ -492,11 +529,22 @@
     def _():
         back_got[...] = jnp.zeros_like(back_got)
 
-    @pl.when(has_next)
-    def _():
-        back_copy(0, 0, TILE, 0).wait_recv()
-
-    place(1, tiles, finish(last, near[1] + decode(back_got[0])))
+    @pl.when(leads)
+    def _():
+        extra_copy(0).wait_recv()
+        effects_hi, effects_lo = split(decode(extra_got[...]))
+        back_copy(0, HALF, 0).wait_recv()
+        back_got[HALF:TILE] = jnp.zeros((TILE - HALF, limit.shape[1]), BF16)
+        extra_copy(1).wait_recv()
+        high, low = split(decode(half_got[...]) * (1.0 / LD_SCALE))
+        term = dot(high, effects_hi) + (dot(high, effects_lo) + dot(low, effects_hi))
+        near[1, HALF:TILE] = near[1, HALF:TILE] + term
+
+    @pl.when(both(has_next, jnp.logical_not(leads)))
+    def _():
+        back_copy(0, TILE, 0).wait_recv()
+
+    place(1, tiles, finish(last, near[1] + decode(back_got[:TILE])))
     out[(last - 1) * TILE : last * TILE] = finish(last - 1, inner + applied(1, last - 1, 2, 1))
     edge = edge + applied(1, last, 1, 1)
 
@@ -506,22 +554,28 @@
 
             @pl.when(has_next)
             def _():
-                back_copy(1, first, size, 1 + first // (3 * QUARTER)).wait_recv()
-
-            combined = edge[rows] + decode_wide(back_got[1, rows])
+                back_copy(TILE + first, size, 1 + first // (3 * QUARTER)).wait_recv()
+
+            combined = edge[rows] + decode_wide(back_got[TILE + first : TILE + first + size])
             out[last * TILE + rows.start : last * TILE + rows.stop] = finish(last, combined, rows)
 
     pl.when(far)(end_last)
 
     @pl.when(has_prev)
     def _():
-        early_copy(2).wait_recv()
         early_copy(1).wait_recv()
-        scale = keep_of(tail_got[pl.ds(0, 1), :])
-        value = decode(early_got[1]) - (1.0 - shrinkage) * (first_term[...] * scale)
-        place(1, 0, soften(value, scale))
-
-    out[:TILE] = finish(0, near[0] + applied(1, 0, 0, 1))
+
+    for k, side in enumerate(sides):
+        @pl.when(has_prev)
+        def _():
+            early_copy(2 + k).wait_recv()
+            scale = keep_of(tail_got[pl.ds(0, 1), :])
+            value = decode(early_got[1, :, side])
+            value = value - (1.0 - shrinkage) * (first_term[:, side] * scale)
+            place(1, 0, soften(value, scale, side), side)
+
+        combined = near[0, :, side] + applied(1, 0, 0, 1, side)
+        out[:TILE, side] = finish(0, combined, every, side)
 
     for k in range(len(peers)):
         diag_copy(k).wait_send()
@@ -538,18 +592,28 @@
     def _():
         geno_sent().wait_send()
         early_sent().wait_send()
-        early_copy(2).wait_send()
-
-    for _, middle, target, slot in routes:
-        @pl.when(var == middle)
-        def _():
-            onward_copy(target, slot).wait_send()
+        early_copy(1).wait_send()
+
+    if routes:
+        @pl.when(var == 0)
+        def _():
+            pltpu.make_async_remote_copy(
+                src_ref=held.at[pl.ds(0, len(routes))], dst_ref=held.at[pl.ds(0, len(routes))],
+                send_sem=held_send, recv_sem=geno_recv.at[1],
+                device_id={"var": following}, device_id_type=MESH,
+            ).wait_send()
 
     pl.when(nearby)(end_last)
 
-    @pl.when(has_prev)
-    def _():
-        back_sent().wait_send()
+    @pl.when(both(has_prev, jnp.logical_not(follows)))
+    def _():
+        back_copy(0, 2 * TILE, 0).wait_send()
+
+    @pl.when(follows)
+    def _():
+        back_copy(0, TILE + HALF, 0).wait_send()
+        for k in range(len(extras)):
+            extra_copy(k).wait_send()
 
 
 def local(genotypes, marginal, start_effects, thresholds):
@@ -589,21 +653,27 @@
             pltpu.VMEM((2, TILE, traits), BF16),
             pltpu.VMEM((8, TILE), F32),
             pltpu.VMEM((8, TILE), F32),
-            pltpu.VMEM((SWEEPS, TILE, traits), BF16),
-            pltpu.VMEM((SWEEPS, TILE, traits), BF16),
+            pltpu.VMEM((SWEEPS * TILE, traits), BF16),
+            pltpu.VMEM((SWEEPS * TILE, traits), BF16),
             pltpu.VMEM((2, TILE, traits), F32),
             pltpu.VMEM((RELAYS, samples // 8, HALF), BF16),
+            pltpu.VMEM((TILE, traits), BF16),
+            pltpu.VMEM((TILE, traits), BF16),
+            pltpu.VMEM((HALF, TILE), BF16),
+            pltpu.VMEM((HALF, TILE), BF16),
             dma((4,)),
             dma,
             dma((4,)),
             dma((others, 2)),
             dma((others, 5)),
             dma((2,)),
+            dma((4,)),
+            dma,
             dma((3,)),
             dma,
-            dma((3,)),
             dma((RELAYS,)),
-            dma((RELAYS,)),
+            dma((2,)),
+            dma((2,)),
         ],
         compiler_params=pltpu.CompilerParams(
             collective_id=0, has_side_effects=True, vmem_limit_bytes=VMEM_BYTES

time: 28.5 us -> 28 us (0.982)
  Pallas kernels: 27.2 us -> 26.7 us
    pallas_call x1, Pallas kernels: 27.2 us -> 26.7 us  [local(): pl.pallas_call(body, out_shape=jax.ShapeDtypeStruct((variants, traits), F...]
where the time goes in v6:
time: 28 us; the launch traced here: 27.9 us
  Pallas kernels  26.7 us (95%)
  local copies, waits for them, and re-layouts  1.15 us (4%)
    pallas_call x1, Pallas kernels, local(): pl.pallas_call(body, out_shape=jax.ShapeDtypeStruct((variants, traits), F...  26.7 us
    unnamed x1, local copies, waits for them, and re-layouts  1.15 us

profile of v6, /device:TPU:1, one launch (start us, length us, event | category | flops | bytes accessed | tf_op | source)
XLA Modules:
  0.0 27.9 jit_solution(17221855845279240401)
XLA Ops:
  0.0 26.7 %shard_map.46 = f32[768,512]{1,0:T(8,128)S(1)} custom-call(bf16[2048,768]{1,0:T(8,128)(2,1)} %geno_hbm.1, f32[768,512]{1,0:T(8,128)} %marg_hbm.1, f32[768,512]{1,0:T(8,128)} %start_hbm.1, f32[1,512]{1,0:T(1,128)} %bitcast.1), custom_call_target="tpu_custom_call" | custom-call | tf_op jit(solution)/shard_map/pallas_call | solution.py:630
  26.8 1.1 %copy.6 = f32[768,512]{1,0:T(8,128)} copy(f32[768,512]{1,0:T(8,128)S(1)} %shard_map.46) | data formatting | bytes 3145728

commit v7 on v6

--- a/solution.py
+++ b/solution.py
@@ -287,12 +287,12 @@
         eff_lo[sweep, begin : begin + TILE, cols] = low
 
     traits = start_hbm.shape[1]
-    width = traits // 2 if traits % 256 == 0 else traits
-    sides = [slice(begin, begin + width) for begin in range(0, traits, width)]
+    turn = max(traits // 512 * 384, traits % 512)
+    sides = [slice(begin, end) for begin, end in ((0, turn), (turn, traits)) if begin < end]
     full = slice(0, traits)
     early = [(early_code.at[0], early_got.at[0], 0), (tail_diag, tail_got, 1)]
     for side in sides:
-        cols = pl.ds(side.start, width)
+        cols = pl.ds(side.start, side.stop - side.start)
         early.append((early_code.at[1, :, cols], early_got.at[1, :, cols], 0))
 
     def early_copy(k):
@@ -488,14 +488,16 @@
     def _():
         first_back(1)
 
-    @pl.when(follows)
-    def _():
-        first_back(1, False)
-
-    @pl.when(has_prev)
-    def _():
+    def take_start():
         early_copy(0).wait_recv()
         place(0, 0, decode(early_got[0]))
+
+    @pl.when(follows)
+    def _():
+        take_start()
+        first_back(1, False)
+
+    pl.when(both(has_prev, jnp.logical_not(follows)))(take_start)
 
     @pl.when(jnp.logical_not(has_prev))
     def _():

time: 28 us -> 27.9 us (level)
    pallas_call x1, Pallas kernels: 26.7 us -> 26.5 us  [local(): pl.pallas_call(body, out_shape=jax.ShapeDtypeStruct((variants, traits), F...]
where the time goes in v7:
time: 27.9 us; the launch traced here: 27.6 us
  Pallas kernels  26.5 us (95%)
  local copies, waits for them, and re-layouts  1.15 us (4%)
    pallas_call x1, Pallas kernels, local(): pl.pallas_call(body, out_shape=jax.ShapeDtypeStruct((variants, traits), F...  26.5 us
    unnamed x1, local copies, waits for them, and re-layouts  1.15 us

profile of v7, /device:TPU:1, one launch (start us, length us, event | category | flops | bytes accessed | tf_op | source)
XLA Modules:
  0.0 27.6 jit_solution(11136687124232654789)
XLA Ops:
  0.0 26.5 %shard_map.46 = f32[768,512]{1,0:T(8,128)S(1)} custom-call(bf16[2048,768]{1,0:T(8,128)(2,1)} %geno_hbm.1, f32[768,512]{1,0:T(8,128)} %marg_hbm.1, f32[768,512]{1,0:T(8,128)} %start_hbm.1, f32[1,512]{1,0:T(1,128)} %bitcast.1), custom_call_target="tpu_custom_call" | custom-call | tf_op jit(solution)/shard_map/pallas_call | solution.py:632
  26.5 1.1 %copy.6 = f32[768,512]{1,0:T(8,128)} copy(f32[768,512]{1,0:T(8,128)S(1)} %shard_map.46) | data formatting | bytes 3145728

commit v8 on v7

--- a/solution.py
+++ b/solution.py
@@ -163,12 +163,13 @@
     cut = depth - depth // 4
     small = depth // 8
     geno_spans = [(0, 0, depth), (1, 0, small), (1, small, cut), (1, cut, depth)]
+    arrivals = (0, 1, 1, 2)
     piece_rows, piece_cols = pl.ds(0, small), pl.ds(last * TILE + HALF, HALF)
 
     def outward_copy(middle, slot):
         return pltpu.make_async_remote_copy(
             src_ref=geno_hbm.at[piece_rows, piece_cols], dst_ref=held.at[slot],
-            send_sem=geno_send, recv_sem=held_recv.at[slot],
+            send_sem=geno_send, recv_sem=held_recv,
             device_id={"var": middle}, device_id_type=MESH,
         )
 
@@ -190,9 +191,17 @@
         return pltpu.make_async_remote_copy(
             src_ref=geno_hbm.at[rows, pl.ds(last * TILE + half * HALF, HALF)],
             dst_ref=halo.at[rows, pl.ds(half * HALF, HALF)],
-            send_sem=geno_send, recv_sem=geno_recv.at[index],
+            send_sem=geno_send, recv_sem=geno_recv.at[arrivals[index]],
             device_id={"var": following}, device_id_type=MESH,
         )
+
+    def geno_taken(half, begin, end, arrival):
+        rows, cols = pl.ds(begin, end - begin), pl.ds(half * HALF, HALF)
+        pltpu.make_async_remote_copy(
+            src_ref=halo.at[rows, cols], dst_ref=halo.at[rows, cols],
+            send_sem=geno_send, recv_sem=geno_recv.at[arrival],
+            device_id={"var": following}, device_id_type=MESH,
+        ).wait_recv()
 
     def geno_sent():
         return pltpu.make_async_remote_copy(
@@ -318,7 +327,7 @@
     def extra_copy(k):
         src, dst = extras[k]
         return pltpu.make_async_remote_copy(
-            src_ref=src, dst_ref=dst, send_sem=extra_send.at[k], recv_sem=extra_recv.at[k],
+            src_ref=src, dst_ref=dst, send_sem=extra_send, recv_sem=extra_recv.at[k],
             device_id={"var": prev}, device_id_type=MESH,
         )
 
@@ -367,9 +376,8 @@
         def _():
             begin = cross_at + half * HALF
             for indices in ((0,),) if half == 0 else ((1, 2), (3,)):
-                for index in indices:
-                    geno_copy(index).wait_recv()
                 first, end = geno_spans[indices[0]][1], geno_spans[indices[-1]][2]
+                geno_taken(half, first, end, arrivals[indices[0]])
                 crossing = gram(
                     halo[first:end, half * HALF : (half + 1) * HALF], geno[first:end, :TILE]
                 )
@@ -384,11 +392,17 @@
 
     for half in halves:
         cross_step(half, nearby)
-    for _, middle, target, slot in routes:
-        @pl.when(var == middle)
-        def _():
-            outward_copy(middle, slot).wait_recv()
-            onward_copy(target, slot).start()
+    if routes:
+        every_slot = held.at[pl.ds(0, len(routes))]
+
+        @pl.when(var == 0)
+        def _():
+            pltpu.make_async_remote_copy(
+                src_ref=every_slot, dst_ref=every_slot, send_sem=held_send, recv_sem=held_recv,
+                device_id={"var": following}, device_id_type=MESH,
+            ).wait_recv()
+            for _, _, target, slot in routes:
+                onward_copy(target, slot).start()
 
     def start_first():
         take_part(0)
@@ -614,8 +628,12 @@
     @pl.when(follows)
     def _():
         back_copy(0, TILE + HALF, 0).wait_send()
-        for k in range(len(extras)):
-            extra_copy(k).wait_send()
+        rows = pl.ds(0, TILE + HALF * TILE // extra_code.shape[1])
+        pltpu.make_async_remote_copy(
+            src_ref=back_code.at[rows], dst_ref=back_got.at[rows],
+            send_sem=extra_send, recv_sem=extra_recv.at[0],
+            device_id={"var": prev}, device_id_type=MESH,
+        ).wait_send()
 
 
 def local(genotypes, marginal, start_effects, thresholds):
@@ -665,7 +683,7 @@
             pltpu.VMEM((HALF, TILE), BF16),
             dma((4,)),
             dma,
-            dma((4,)),
+            dma((3,)),
             dma((others, 2)),
             dma((others, 5)),
             dma((2,)),
@@ -673,8 +691,8 @@
             dma,
             dma((3,)),
             dma,
-            dma((RELAYS,)),
-            dma((2,)),
+            dma,
+            dma,
             dma((2,)),
         ],
         compiler_params=pltpu.CompilerParams(

time: 27.9 us -> 27.8 us (level)
  no operation moved by 1% of the time
where the time goes in v8:
time: 27.8 us; the launch traced here: 27.6 us
  Pallas kernels  26.4 us (95%)
  local copies, waits for them, and re-layouts  1.15 us (4%)
    pallas_call x1, Pallas kernels, local(): pl.pallas_call(body, out_shape=jax.ShapeDtypeStruct((variants, traits), F...  26.4 us
    unnamed x1, local copies, waits for them, and re-layouts  1.15 us

profile of v8, /device:TPU:1, one launch (start us, length us, event | category | flops | bytes accessed | tf_op | source)
XLA Modules:
  0.0 27.6 jit_solution(3104588531081162829)
XLA Ops:
  0.0 26.4 %shard_map.46 = f32[768,512]{1,0:T(8,128)S(1)} custom-call(bf16[2048,768]{1,0:T(8,128)(2,1)} %geno_hbm.1, f32[768,512]{1,0:T(8,128)} %marg_hbm.1, f32[768,512]{1,0:T(8,128)} %start_hbm.1, f32[1,512]{1,0:T(1,128)} %bitcast.1), custom_call_target="tpu_custom_call" | custom-call | tf_op jit(solution)/shard_map/pallas_call | solution.py:650
  26.4 1.1 %copy.6 = f32[768,512]{1,0:T(8,128)} copy(f32[768,512]{1,0:T(8,128)S(1)} %shard_map.46) | data formatting | bytes 3145728
